TPU v7x, 256 devices: a whole 4x4x8 slice. The times are simulated.
256 devices in a mesh: tm: 8 (over z), height: 16 (over x, y), width: 2 (over core).
Axes of the slice: x: 4, y: 4, z: 8, core: 2. Of those that a mesh axis runs over, the one named last changes fastest.
Arguments:
- video: bfloat16 [2, 128, 16, 256, 128], P('width', ('tm', 'height')), may hold values from -6 to 6
- out_grad: bfloat16 [2, 128, 16, 256, 128], P('width', None, 'tm', 'height'), may hold values from -6 to 6
- lengths: int32 [4], replicated, may hold values from 1 to 6, 16 in all
- temporal_weight: bfloat16 [3, 128, 128], replicated, may hold values from -0.3125 to 0.3125
- spatial_weight: bfloat16 [3, 3, 128, 128], replicated, may hold values from -0.1875 to 0.1875
Outputs:
- video_grad: bfloat16 [2, 128, 16, 256, 128], P('width', ('tm', 'height'))
- temporal_grad: float32 [3, 128, 128], replicated
- spatial_grad: float32 [3, 3, 128, 128], replicated
Inputs may be any that keep to these rules, and one draw needn't show every extreme that they name: The 4 clips lie end to end in frame order, their lengths sum to 16, and the longest clip has exactly 6 frames.
All inputs are finite; a program needn't handle non-finite values.
Results may differ from a plain program's by a relative error of at most 0.008.
Values may be sent and summed in bfloat16 or wider, within the bound.
A program may use at most 128 MiB of HBM per device.

v0:
```python
import jax
import jax.numpy as jnp
from jax import lax
from jax.sharding import PartitionSpec as P


def with_halo(cells, sides, width):
    for axis, dim in sides:
        count = lax.axis_size(axis)
        ends = count - 1
        head = lax.slice_in_dim(cells, 0, width, axis=dim)
        tail = lax.slice_in_dim(cells, cells.shape[dim] - width, cells.shape[dim], axis=dim)
        cells = jnp.concatenate(
            [
                lax.ppermute(tail, axis, [(i, (i + 1) % count) for i in range(ends)]),
                cells,
                lax.ppermute(head, axis, [((i + 1) % count, i) for i in range(ends)]),
            ],
            axis=dim,
        )
    return cells


def frame_masks(lengths, frames):
    ends = jnp.cumsum(lengths, dtype=jnp.int32)
    starts = ends - lengths
    frame_index = jnp.arange(frames, dtype=jnp.int32)
    inside = (frame_index[:, None] >= starts[None, :]) & (frame_index[:, None] < ends[None, :])
    first = jnp.sum(jnp.where(inside, starts[None, :], 0), axis=1, dtype=jnp.int32)
    return jnp.stack([frame_index - lag >= first for lag in range(3)]).astype(jnp.bfloat16)


def silu_slope(pre, grads):
    sig = jax.nn.sigmoid(pre)
    return grads.astype(jnp.float32) * sig * (1.0 + pre * (1.0 - sig))


def flatten(block):
    return block.reshape(-1, block.shape[-1])


def spatial_forward(padded, weights, cols, rows):
    total = None
    for row_off in range(3):
        for col_off in range(3):
            piece = flatten(padded[col_off : col_off + cols, :, row_off : row_off + rows])
            term = jnp.dot(piece, weights[row_off, col_off], preferred_element_type=jnp.float32)
            total = term if total is None else total + term
    return total


def shards(video, out_grad, lengths, temporal_weight, spatial_weight):
    width_loc = video.shape[1]
    frames = video.shape[2]
    rows = video.shape[3]
    chans = video.shape[4]
    n_tm = lax.axis_size("tm")
    n_height = lax.axis_size("height")
    frames_dev = frames // n_tm
    rows_dev = rows // n_height
    cols_half = out_grad.shape[1]
    total_cols = cols_half * lax.axis_size("width")
    masks = frame_masks(lengths, frames)
    local_video = video[0]
    padded_video = jnp.pad(local_video, ((0, 0), (2, 0), (0, 0), (0, 0)))
    taps = [
        padded_video[:, 2 - lag : 2 - lag + frames] * masks[lag][None, :, None, None]
        for lag in range(3)
    ]
    total = None
    for lag in range(3):
        term = jnp.dot(flatten(taps[lag]), temporal_weight[lag], preferred_element_type=jnp.float32)
        total = term if total is None else total + term
    act_time = total.astype(jnp.bfloat16).reshape(local_video.shape)
    arranged = act_time.reshape(width_loc, n_tm, frames_dev, n_height, rows_dev, chans)
    arranged = arranged.transpose(1, 3, 0, 2, 4, 5).reshape(
        n_tm * n_height * width_loc, frames_dev, rows_dev, chans
    )
    act_space = lax.all_to_all(arranged, ("tm", "height"), split_axis=0, concat_axis=0, tiled=True)
    grad_space = out_grad[0]
    padded_act = with_halo(act_space, (("height", 2), ("width", 0)), 1)
    pre = spatial_forward(padded_act, spatial_weight, cols_half, rows_dev)
    delta = silu_slope(pre, flatten(grad_space)).astype(jnp.bfloat16).reshape(act_space.shape)
    padded_delta = with_halo(delta, (("height", 2), ("width", 0)), 1)
    flat_delta = flatten(delta)
    back = None
    spatial_terms = []
    for row_off in range(3):
        line = []
        for col_off in range(3):
            piece = flatten(
                padded_delta[
                    2 - col_off : 2 - col_off + cols_half, :, 2 - row_off : 2 - row_off + rows_dev
                ]
            )
            term = jnp.dot(
                piece, spatial_weight[row_off, col_off].T, preferred_element_type=jnp.float32
            )
            back = term if back is None else back + term
            source = flatten(
                padded_act[col_off : col_off + cols_half, :, row_off : row_off + rows_dev]
            )
            line.append(
                lax.dot_general(
                    source, flat_delta, (((0,), (0,)), ((), ())), preferred_element_type=jnp.float32
                )
            )
        spatial_terms.append(jnp.stack(line))
    spatial_local = jnp.stack(spatial_terms)
    grad_act_space = back.astype(jnp.bfloat16).reshape(act_space.shape)
    received = lax.all_to_all(
        grad_act_space, ("tm", "height"), split_axis=0, concat_axis=0, tiled=True
    )
    received = received.reshape(n_tm, n_height, width_loc, frames_dev, rows_dev, chans)
    grad_time = received.transpose(2, 0, 3, 1, 4, 5).reshape(width_loc, frames, rows, chans)
    flat_grad = flatten(grad_time)
    frame_total = None
    temporal_terms = []
    for lag in range(3):
        temporal_terms.append(
            lax.dot_general(
                flatten(taps[lag]),
                flat_grad,
                (((0,), (0,)), ((), ())),
                preferred_element_type=jnp.float32,
            )
        )
        masked = flatten(grad_time * masks[lag][None, :, None, None])
        product = jnp.dot(
            masked, temporal_weight[lag].T, preferred_element_type=jnp.float32
        ).reshape(grad_time.shape)
        moved = jnp.pad(product[:, lag:], ((0, 0), (0, lag), (0, 0), (0, 0)))
        frame_total = moved if frame_total is None else frame_total + moved
    temporal_local = jnp.stack(temporal_terms)
    video_grad = frame_total.astype(jnp.bfloat16)[None]
    scale = float(frames * rows * total_cols) ** (-0.5)
    temporal_grad, spatial_grad = lax.psum(
        (temporal_local * scale, spatial_local * scale), ("tm", "height", "width")
    )
    return (video_grad, temporal_grad, spatial_grad)


def solution(mesh):
    placed = (
        P("width", ("tm", "height"), None, None, None),
        P("width", None, "tm", "height", None),
        P(),
        P(),
        P(),
    )
    return jax.shard_map(
        shards,
        mesh=mesh,
        in_specs=placed,
        out_specs=(P("width", ("tm", "height"), None, None, None), P(), P()),
        check_vma=False,
    )
```

profile of v0, /device:TPU:1, one launch (start us, length us, event | category | flops | bytes accessed | tf_op | source)
XLA Modules:
  0.0 413.3 jit_solution(14738831127467204281)
XLA Ops:
  7.2 0.9 reduce-window.8
  8.0 0.7 bitcast_subtract_fusion
  8.8 1.4 broadcast_multiply_fusion
  10.7 1.2 copy-done.15
  12.5 0.5 copy-done.11
  13.3 0.4 fusion.2
  14.0 44.8 %all_to_all.10 = bf16[128,2,16,128]{3,2,1,0:T(8,128)(2,1)S(1)} all-to-all(bf16[128,2,16,128]{3,2,1,0:T(8,128)(2,1)S(1)} %bitcast.249), channel_id=1, replica_groups=mesh['tm'=8,'height'=16,'width'=2] {'tm','height'}, dimensions={0} | all-to-all | bytes 2097152 | tf_op jit(solution)/shard_map/all_to_all | solution.py:79
  58.9 2.2 collective-permute-start
  61.2 1.3 collective-permute-start.1
  63.1 3.8 collective-permute-done.1
  66.9 1.3 collective-permute-start.2
  68.2 6.8 %collective-permute-start.3 = (bf16[1,2,18,128]{3,2,1,0:T(8,128)(2,1)S(1)}, bf16[1,2,18,128]{3,2,1,0:T(8,128)(2,1)S(1)}, u32[]{:S(2)}, u32[]{:S(2)}) collective-permute-start(bf16[1,2,18,128]{3,2,1,0:T(8,128)(2,1)S(1)} %get-tuple-element.27), channel_id=1, source_target_pairs={{1,0},{3,2},{5,4},{7,6},{9,8},{11,10},{13,12},{15,14},{17,16},{19,... | collective-permute-start | bytes 27656 | tf_op jit(solution)/shard_map/ppermute | solution.py:17
  75.0 1.0 pad_maximum_fusion.4
  76.1 0.4 fusion.32
  76.5 2.0 maximum_maximum_fusion
  78.5 1.3 fusion.67
  82.1 0.4 convolution_add_fusion.11
  83.0 0.4 convolution_add_fusion.9
  83.4 0.4 convolution_add_fusion.8
  83.8 0.8 copy-done.20
  84.6 1.1 fusion.5
  85.9 1.8 collective-permute-start.4
  87.7 1.5 collective-permute-start.5
  89.2 0.5 convolution_bitcast_fusion.9
  89.6 1.2 collective-permute-done.4
  90.9 4.6 %collective-permute-done.5 = bf16[128,2,1,128]{3,2,1,0:T(2,128)(2,1)S(1)} collective-permute-done((bf16[128,2,1,128]{3,2,1,0:T(2,128)(2,1)S(1)}, bf16[128,2,1,128]{3,2,1,0:T(2,128)(2,1)S(1)}, u32[]{:S(2)}, u32[]{:S(2)}) %collective-permute-start.5) | collective-permute-done | bytes 65568 | tf_op jit(solution)/shard_map/ppermute | solution.py:17
  95.4 2.4 collective-permute-start.6
  97.8 1.3 collective-permute-start.7
  99.1 1.0 pad_maximum_fusion.2
  100.2 0.4 fusion.30
  100.9 2.0 pad_maximum_fusion.1
  102.9 0.6 fusion.65
  103.5 0.6 fusion.66
  104.2 0.4 convolution_add_fusion.6
  104.6 0.4 convolution_add_fusion.5
  105.0 0.4 convolution_add_fusion.4
  105.5 0.4 convolution_add_fusion.3
  105.9 0.4 fusion.14
  106.3 0.4 convolution_add_fusion.2
  106.8 0.4 convolution_add_fusion.1
  107.2 1.4 fusion.3
  108.7 12.8 %all-to-all-start.1 = ((bf16[128,2,16,128]{3,2,1,0:T(8,128)(2,1)}), bf16[128,2,16,128]{3,2,1,0:T(8,128)(2,1)}, u32[]{:S(2)}, u32[]{:S(2)}) async-start(bf16[128,2,16,128]{3,2,1,0:T(8,128)(2,1)} %bitcast.251), calls=%async_computation.1 | async-start | bytes 2097152 | tf_op jit(solution)/shard_map/all_to_all | solution.py:111
  121.7 1.8 convolution_bitcast_fusion.10
  123.6 0.5 convolution_bitcast_fusion.8
  124.1 0.5 convolution_bitcast_fusion.5
  124.8 0.5 convolution_bitcast_fusion.7
  125.3 0.5 convolution_bitcast_fusion.6
  126.0 0.5 convolution_bitcast_fusion.3
  126.6 0.5 convolution_bitcast_fusion.2
  127.1 0.5 convolution_bitcast_fusion.4
  127.6 0.9 maximum_multiply_fusion
  128.5 21.0 %all-to-all-done.1 = bf16[128,2,16,128]{3,2,1,0:T(8,128)(2,1)} async-done(((bf16[128,2,16,128]{3,2,1,0:T(8,128)(2,1)}), bf16[128,2,16,128]{3,2,1,0:T(8,128)(2,1)}, u32[]{:S(2)}, u32[]{:S(2)}) %all-to-all-start.1) | async-done | bytes 1048608 | tf_op jit(solution)/shard_map/all_to_all | solution.py:111
  149.4 1.5 copy.12
  151.0 0.5 convolution_bitcast_fusion.11
  151.5 0.5 convolution_bitcast_fusion.12
  152.2 0.5 convolution_bitcast_fusion.13
  152.7 0.7 maximum_multiply_fusion.1
  153.4 1.5 bitcast_multiply_fusion.2
  154.9 0.4 convolution_bitcast_fusion.1
  155.6 0.4 convolution_bitcast_fusion
  156.1 1.4 fusion.8
  157.6 245.3 %all-reduce.6.cloned.1.call-done = (f32[3,128,128]{2,1,0:T(8,128)}, f32[3,3,128,128]{3,2,1,0:T(8,128)}) async-done(((f32[3,128,128]{2,1,0:T(8,128)}, f32[3,3,128,128]{3,2,1,0:T(8,128)}), (f32[3,128,128]{2,1,0:T(8,128)}, f32[3,3,128,128]{3,2,1,0:T(8,128)})) %all-reduce.6.cloned.1.call-update) | async-done | bytes 786448 | tf_op jit(solution)/shard_map/psum | solution.py:137
  402.9 1.6 copy.18
  404.5 1.9 copy.19
  (70 shorter events, 7.1 us)
Async XLA Ops:
  7.2 3.1 copy-start.19
  10.2 1.8 copy-start.9
  10.2 1.6 copy-start.15
  12.0 1.0 copy-start.11
  12.0 1.3 copy-start.13
  58.9 4.2 %collective-permute-start = (bf16[128,2,1,128]{3,2,1,0:T(2,128)(2,1)S(1)}, bf16[128,2,1,128]{3,2,1,0:T(2,128)(2,1)S(1)}, u32[]{:S(2)}, u32[]{:S(2)}) collective-permute-start(bf16[128,2,1,128]{3,2,1,0:T(2,128)(2,1)S(1)} %get-tuple-element.37), channel_id=1, source_target_pairs={{0,2},{2,4},{4,6},{6,8},{8,10},{10,12},{12,14},{14,16},{16,18},{18... | collective-permute-start | bytes 196616 | tf_op jit(solution)/shard_map/ppermute | solution.py:15
  61.2 5.7 %collective-permute-start.1 = (bf16[128,2,1,128]{3,2,1,0:T(2,128)(2,1)S(1)}, bf16[128,2,1,128]{3,2,1,0:T(2,128)(2,1)S(1)}, u32[]{:S(2)}, u32[]{:S(2)}) collective-permute-start(bf16[128,2,1,128]{3,2,1,0:T(2,128)(2,1)S(1)} %get-tuple-element.38), channel_id=1, source_target_pairs={{2,0},{4,2},{6,4},{8,6},{10,8},{12,10},{14,12},{16,14},{18,16},{20... | collective-permute-start | bytes 196616 | tf_op jit(solution)/shard_map/ppermute | solution.py:17
  62.7 13.3 %copy-start.18 = (bf16[3,3,128,128]{3,2,1,0:T(8,128)(2,1)S(1)}, bf16[3,3,128,128]{3,2,1,0:T(8,128)(2,1)}, u32[]{:S(2)}) copy-start(bf16[3,3,128,128]{3,2,1,0:T(8,128)(2,1)} %param.9) | copy-start | bytes 884740
  66.9 9.6 %collective-permute-start.2 = (bf16[1,2,18,128]{3,2,1,0:T(8,128)(2,1)S(1)}, bf16[1,2,18,128]{3,2,1,0:T(8,128)(2,1)S(1)}, u32[]{:S(2)}, u32[]{:S(2)}) collective-permute-start(bf16[1,2,18,128]{3,2,1,0:T(8,128)(2,1)S(1)} %get-tuple-element.26), channel_id=1, source_target_pairs={{0,1},{2,3},{4,5},{6,7},{8,9},{10,11},{12,13},{14,15},{16,17},{18,... | collective-permute-start | bytes 27656 | tf_op jit(solution)/shard_map/ppermute | solution.py:15
  68.2 8.3 %collective-permute-start.3 = (bf16[1,2,18,128]{3,2,1,0:T(8,128)(2,1)S(1)}, bf16[1,2,18,128]{3,2,1,0:T(8,128)(2,1)S(1)}, u32[]{:S(2)}, u32[]{:S(2)}) collective-permute-start(bf16[1,2,18,128]{3,2,1,0:T(8,128)(2,1)S(1)} %get-tuple-element.27), channel_id=1, source_target_pairs={{1,0},{3,2},{5,4},{7,6},{9,8},{11,10},{13,12},{15,14},{17,16},{19,... | collective-permute-start | bytes 27656 | tf_op jit(solution)/shard_map/ppermute | solution.py:17
  76.1 7.8 %copy-start.16 = (bf16[128,2,16,128]{3,2,1,0:T(8,128)(2,1)}, bf16[128,2,16,128]{3,2,1,0:T(8,128)(2,1)S(1)}, u32[]{:S(2)}) copy-start(bf16[128,2,16,128]{3,2,1,0:T(8,128)(2,1)S(1)} %get-tuple-element.35) | copy-start | bytes 3145732
  79.9 1.0 copy-start
  79.9 1.4 copy-start.8
  79.9 1.8 copy-start.6
  79.9 2.2 copy-start.2
  79.9 3.0 copy-start.4
  83.4 1.2 copy-start.20
  85.9 5.0 %collective-permute-start.4 = (bf16[128,2,1,128]{3,2,1,0:T(2,128)(2,1)S(1)}, bf16[128,2,1,128]{3,2,1,0:T(2,128)(2,1)S(1)}, u32[]{:S(2)}, u32[]{:S(2)}) collective-permute-start(bf16[128,2,1,128]{3,2,1,0:T(2,128)(2,1)S(1)} %get-tuple-element.33), channel_id=1, source_target_pairs={{0,2},{2,4},{4,6},{6,8},{8,10},{10,12},{12,14},{14,16},{16,18},{18... | collective-permute-start | bytes 196616 | tf_op jit(solution)/shard_map/ppermute | solution.py:15
  87.7 7.7 %collective-permute-start.5 = (bf16[128,2,1,128]{3,2,1,0:T(2,128)(2,1)S(1)}, bf16[128,2,1,128]{3,2,1,0:T(2,128)(2,1)S(1)}, u32[]{:S(2)}, u32[]{:S(2)}) collective-permute-start(bf16[128,2,1,128]{3,2,1,0:T(2,128)(2,1)S(1)} %get-tuple-element.34), channel_id=1, source_target_pairs={{2,0},{4,2},{6,4},{8,6},{10,8},{12,10},{14,12},{16,14},{18,16},{20... | collective-permute-start | bytes 196616 | tf_op jit(solution)/shard_map/ppermute | solution.py:17
  95.4 5.2 %collective-permute-start.6 = (bf16[1,2,18,128]{3,2,1,0:T(8,128)(2,1)S(1)}, bf16[1,2,18,128]{3,2,1,0:T(8,128)(2,1)S(1)}, u32[]{:S(2)}, u32[]{:S(2)}) collective-permute-start(bf16[1,2,18,128]{3,2,1,0:T(8,128)(2,1)S(1)} %get-tuple-element.22), channel_id=1, source_target_pairs={{1,0},{3,2},{5,4},{7,6},{9,8},{11,10},{13,12},{15,14},{17,16},{19,... | collective-permute-start | bytes 27656 | tf_op jit(solution)/shard_map/ppermute | solution.py:17
  97.8 3.1 collective-permute-start.7
  108.7 40.8 %all-to-all-start.1 = ((bf16[128,2,16,128]{3,2,1,0:T(8,128)(2,1)}), bf16[128,2,16,128]{3,2,1,0:T(8,128)(2,1)}, u32[]{:S(2)}, u32[]{:S(2)}) async-start(bf16[128,2,16,128]{3,2,1,0:T(8,128)(2,1)} %bitcast.251), calls=%async_computation.1 | async-start | bytes 2097152 | tf_op jit(solution)/shard_map/all_to_all | solution.py:111
  121.4 281.5 %all-reduce.6.cloned.1.call-start = ((), (), s32[]{:S(2)}) async-start(), calls=%async_computation.2 | async-start | bytes 1572864 | tf_op jit(solution)/shard_map/psum | solution.py:137
  121.7 1.9 copy-start.7
  121.7 2.4 copy-start.5
  123.6 1.2 copy-start.3
  124.8 1.2 copy-start.17
  125.3 1.3 copy-start.1
  127.6 23.4 %copy-start.14 = (bf16[1,16,256,128]{3,2,1,0:T(8,128)(2,1)S(1)}, bf16[1,16,256,128]{3,2,1,0:T(8,128)(2,1)}, u32[]{:S(2)}) copy-start(bf16[1,16,256,128]{3,2,1,0:T(8,128)(2,1)} %copy-done.13) | copy-start | bytes 3145732
  149.4 2.0 copy-start.12
  151.0 1.2 copy-start.10
Sparse Core Ops, SparseCore 0:
  153.5 249.3 all-reduce.5
where the time goes:
time: 415 us; the launch traced here: 413 us
  waiting for transfers between devices  277 us (67%)
  blocking collectives  44.8 us (11%)
  starting transfers between devices  31.6 us (8%)
  matrix products  20 us (5%)
  between operations  14.7 us (4%)
  local copies, waits for them, and re-layouts  13.4 us (3%)
  other arithmetic  12.4 us (3%)
    psum x1, waiting for transfers between devices, shards(): lax.psum((temporal_local * scale, spatial_local * scale), ('tm', 'height'...  245 us
    all_to_all x1, blocking collectives, shards(): lax.all_to_all(arranged, ('tm', 'height'), split_axis=0, concat_axis=0, t...  44.8 us
    all_to_all x1, waiting for transfers between devices, shards(): lax.all_to_all(grad_act_space, ('tm', 'height'), split_axis=0, concat_axi...  21 us
    all_to_all x1, starting transfers between devices, shards(): lax.all_to_all(grad_act_space, ('tm', 'height'), split_axis=0, concat_axi...  12.8 us
    ppermute x4, starting transfers between devices, with_halo(): lax.ppermute(head, axis, [((i + 1) % count, i) for i in range(ends)])  12 us
    ppermute x4, waiting for transfers between devices, with_halo(): lax.ppermute(head, axis, [((i + 1) % count, i) for i in range(ends)])  8.36 us
  transfers between devices with their start and end apart: 10, of which 7 were waited for; matrix products, arithmetic and copies ran while one was open for 3% of the time, Pallas kernels for 0%

commit v1 on v0

v1 whole, which is shorter than its diff:
```python
import functools

import jax
import jax.numpy as jnp
from jax import lax
from jax.experimental import pallas as pl
from jax.experimental.pallas import tpu as pltpu
from jax.sharding import PartitionSpec as P

MESH = pl.DeviceIdType.MESH


def reduce_kernel(n_tm, n_h, x_ref, o_ref, pair_buf, half, h_buf, z_buf, pair_sem, h_send, h_recv, z_send, z_recv, g_send, g_recv, f_send, f_recv):
    tm = lax.axis_index("tm")
    h = lax.axis_index("height")
    w = lax.axis_index("width")
    rows = x_ref.shape[0]
    half_rows = rows // 2
    piece = half_rows // n_h
    barrier = pltpu.get_barrier_semaphore()
    pl.semaphore_signal(barrier, inc=1, device_id=(tm, h, 1 - w), device_id_type=MESH)

    def greet_h(d, _):
        pl.semaphore_signal(barrier, inc=1, device_id=(tm, (h + d) % n_h, w), device_id_type=MESH)
        return _

    def greet_z(d, _):
        pl.semaphore_signal(barrier, inc=1, device_id=((tm + d) % n_tm, h, w), device_id_type=MESH)
        return _

    lax.fori_loop(1, n_h, greet_h, 0)
    lax.fori_loop(1, n_tm, greet_z, 0)
    pl.semaphore_wait(barrier, 1 + n_h - 1 + n_tm - 1)

    other = pl.multiple_of((1 - w) * half_rows, half_rows)
    mine = pl.multiple_of(w * half_rows, half_rows)
    pair = pltpu.make_async_remote_copy(
        src_ref=x_ref.at[pl.ds(other, half_rows)], dst_ref=pair_buf, send_sem=pair_sem.at[0], recv_sem=pair_sem.at[1],
        device_id=(tm, h, 1 - w), device_id_type=MESH)
    pair.start()
    pair.wait()
    half[...] = x_ref[pl.ds(mine, half_rows), :] + pair_buf[...]

    def h_copy(d):
        to = (h + d) % n_h
        return pltpu.make_async_remote_copy(
            src_ref=half.at[pl.ds(pl.multiple_of(to * piece, 8), piece)], dst_ref=h_buf.at[d],
            send_sem=h_send.at[d], recv_sem=h_recv.at[d], device_id=(tm, to, w), device_id_type=MESH)

    def go(copy):
        def body(d, _):
            copy(d).start()
            return _
        return body

    def done(copy):
        def body(d, _):
            copy(d).wait()
            return _
        return body

    lax.fori_loop(1, n_h, go(h_copy), 0)
    lax.fori_loop(1, n_h, done(h_copy), 0)
    h_buf[0] = half[pl.ds(pl.multiple_of(h * piece, 8), piece), :]
    total = h_buf[0]
    for d in range(1, n_h):
        total = total + h_buf[d]
    z_buf[tm] = total

    def z_copy(d):
        to = (tm + d) % n_tm
        return pltpu.make_async_remote_copy(
            src_ref=z_buf.at[tm], dst_ref=z_buf.at[tm],
            send_sem=z_send.at[d], recv_sem=z_recv.at[d], device_id=(to, h, w), device_id_type=MESH)

    lax.fori_loop(1, n_tm, go(z_copy), 0)
    lax.fori_loop(1, n_tm, done(z_copy), 0)
    total = z_buf[0]
    for t in range(1, n_tm):
        total = total + z_buf[t]
    here = pl.ds(pl.multiple_of(mine + h * piece, 8), piece)
    o_ref[here, :] = total

    def g_copy(d):
        to = (h + d) % n_h
        return pltpu.make_async_remote_copy(
            src_ref=o_ref.at[here], dst_ref=o_ref.at[here],
            send_sem=g_send.at[d], recv_sem=g_recv.at[d], device_id=(tm, to, w), device_id_type=MESH)

    def f_copy(d):
        owner = (h + n_h - d) % n_h
        there = pl.ds(pl.multiple_of(mine + owner * piece, 8), piece)
        return pltpu.make_async_remote_copy(
            src_ref=o_ref.at[there], dst_ref=o_ref.at[there],
            send_sem=f_send.at[d], recv_sem=f_recv.at[d], device_id=(tm, h, 1 - w), device_id_type=MESH)

    lax.fori_loop(1, n_h, go(g_copy), 0)
    f_copy(0).start()

    def forward(d, _):
        g_copy(d).wait()
        f_copy(d).start()
        return _

    lax.fori_loop(1, n_h, forward, 0)
    lax.fori_loop(0, n_h, done(f_copy), 0)


def all_reduce(x, n_tm, n_h):
    rows, lanes = x.shape
    half_rows = rows // 2
    piece = half_rows // n_h
    dma = pltpu.SemaphoreType.DMA
    return pl.pallas_call(
        functools.partial(reduce_kernel, n_tm, n_h),
        out_shape=jax.ShapeDtypeStruct((rows, lanes), jnp.float32),
        in_specs=[pl.BlockSpec(memory_space=pltpu.VMEM)],
        out_specs=pl.BlockSpec(memory_space=pltpu.VMEM),
        scratch_shapes=[
            pltpu.VMEM((half_rows, lanes), jnp.float32),
            pltpu.VMEM((half_rows, lanes), jnp.float32),
            pltpu.VMEM((n_h, piece, lanes), jnp.float32),
            pltpu.VMEM((n_tm, piece, lanes), jnp.float32),
            dma((2,)), dma((n_h,)), dma((n_h,)), dma((n_tm,)), dma((n_tm,)), dma((n_h,)), dma((n_h,)), dma((n_h,)), dma((n_h,)),
        ],
        compiler_params=pltpu.CompilerParams(collective_id=0, has_side_effects=True),
    )(x)


def with_halo(cells, n_tm, n_w):
    def joined(cells, axis, order, dim):
        head = lax.slice_in_dim(cells, 0, 1, axis=dim)
        tail = lax.slice_in_dim(cells, cells.shape[dim] - 1, cells.shape[dim], axis=dim)
        before = lax.ppermute(tail, axis, list(zip(order[:-1], order[1:])))
        after = lax.ppermute(head, axis, list(zip(order[1:], order[:-1])))
        return jnp.concatenate([before, cells, after], axis=dim)

    cells = joined(cells, "height", list(range(lax.axis_size("height"))), 2)
    return joined(cells, ("tm", "width"), [t * n_w + w for w in range(n_w) for t in range(n_tm)], 0)


def frame_masks(lengths, frames):
    ends = jnp.cumsum(lengths, dtype=jnp.int32)
    starts = ends - lengths
    frame_index = jnp.arange(frames, dtype=jnp.int32)
    inside = (frame_index[:, None] >= starts[None, :]) & (frame_index[:, None] < ends[None, :])
    first = jnp.sum(jnp.where(inside, starts[None, :], 0), axis=1, dtype=jnp.int32)
    return jnp.stack([frame_index - lag >= first for lag in range(3)]).astype(jnp.bfloat16)


def silu_slope(pre, grads):
    sig = jax.nn.sigmoid(pre)
    return grads.astype(jnp.float32) * sig * (1.0 + pre * (1.0 - sig))


def flatten(block):
    return block.reshape(-1, block.shape[-1])


def shards(video, out_grad, lengths, temporal_weight, spatial_weight):
    frames = video.shape[2]
    rows = video.shape[3]
    chans = video.shape[4]
    n_tm = lax.axis_size("tm")
    n_height = lax.axis_size("height")
    frames_dev = frames // n_tm
    rows_dev = rows // n_height
    cols_half = out_grad.shape[1]
    cols_dev = cols_half // n_tm
    total_cols = cols_half * lax.axis_size("width")
    masks = frame_masks(lengths, frames)
    bands = video[0, 0].reshape(frames, n_height, rows_dev, chans).transpose(1, 0, 2, 3)
    tile = lax.all_to_all(bands, "height", split_axis=0, concat_axis=0, tiled=True)
    grads = lax.all_to_all(out_grad[0], "tm", split_axis=0, concat_axis=0, tiled=True)
    grads = grads.reshape(n_tm, cols_dev, frames_dev, rows_dev, chans).transpose(1, 0, 2, 3, 4).reshape(cols_dev, frames, rows_dev, chans)
    padded = jnp.pad(tile, ((0, 0), (2, 0), (0, 0), (0, 0)))
    taps = [padded[:, 2 - lag : 2 - lag + frames] * masks[lag][None, :, None, None] for lag in range(3)]
    total = None
    for lag in range(3):
        term = jnp.dot(flatten(taps[lag]), temporal_weight[lag], preferred_element_type=jnp.float32)
        total = term if total is None else total + term
    act = total.astype(jnp.bfloat16).reshape(tile.shape)
    n_width = lax.axis_size("width")
    padded_act = with_halo(act, n_tm, n_width)
    pre = None
    for row_off in range(3):
        for col_off in range(3):
            piece = flatten(padded_act[col_off : col_off + cols_dev, :, row_off : row_off + rows_dev])
            term = jnp.dot(piece, spatial_weight[row_off, col_off], preferred_element_type=jnp.float32)
            pre = term if pre is None else pre + term
    delta = silu_slope(pre, flatten(grads)).astype(jnp.bfloat16).reshape(tile.shape)
    padded_delta = with_halo(delta, n_tm, n_width)
    flat_delta = flatten(delta)
    back = None
    spatial_terms = []
    for row_off in range(3):
        for col_off in range(3):
            piece = flatten(padded_delta[2 - col_off : 2 - col_off + cols_dev, :, 2 - row_off : 2 - row_off + rows_dev])
            term = jnp.dot(piece, spatial_weight[row_off, col_off].T, preferred_element_type=jnp.float32)
            back = term if back is None else back + term
            source = flatten(padded_act[col_off : col_off + cols_dev, :, row_off : row_off + rows_dev])
            spatial_terms.append(
                lax.dot_general(source, flat_delta, (((0,), (0,)), ((), ())), preferred_element_type=jnp.float32)
            )
    act_grad = back.astype(jnp.bfloat16).reshape(tile.shape)
    flat_grad = flatten(act_grad)
    frame_total = None
    temporal_terms = []
    for lag in range(3):
        temporal_terms.append(
            lax.dot_general(flatten(taps[lag]), flat_grad, (((0,), (0,)), ((), ())), preferred_element_type=jnp.float32)
        )
        masked = flatten(act_grad * masks[lag][None, :, None, None])
        product = jnp.dot(masked, temporal_weight[lag].T, preferred_element_type=jnp.float32).reshape(tile.shape)
        moved = jnp.pad(product[:, lag:], ((0, 0), (0, lag), (0, 0), (0, 0)))
        frame_total = moved if frame_total is None else frame_total + moved
    scale = float(frames * rows * total_cols) ** (-0.5)
    terms = jnp.concatenate(spatial_terms + temporal_terms, axis=0) * scale
    summed = all_reduce(terms, n_tm, n_height)
    moved = lax.all_to_all(frame_total.astype(jnp.bfloat16), "height", split_axis=0, concat_axis=0, tiled=True)
    video_grad = moved.transpose(1, 0, 2, 3).reshape(1, 1, frames, rows, chans)
    return (
        video_grad,
        summed[9 * chans :].reshape(3, chans, chans),
        summed[: 9 * chans].reshape(3, 3, chans, chans),
    )


def solution(mesh):
    placed = (
        P("width", ("tm", "height"), None, None, None),
        P("width", None, "tm", "height", None),
        P(),
        P(),
        P(),
    )
    return jax.shard_map(
        shards,
        mesh=mesh,
        in_specs=placed,
        out_specs=(P("width", ("tm", "height"), None, None, None), P(), P()),
        check_vma=False,
    )
```

time: 415 us -> 182 us (0.44)
  waiting for transfers between devices: 277 us -> 27.6 us
  blocking collectives: 44.8 us -> 0 us
  Pallas kernels: 0 us -> 36.1 us
  starting transfers between devices: 31.6 us -> 56.6 us
  between operations: 14.7 us -> 1.22 us
  local copies, waits for them, and re-layouts: 13.4 us -> 23.2 us
  matrix products: 20 us -> 26.1 us
    psum x1 -> x0, waiting for transfers between devices: 245 us -> none  [shards(): lax.psum((temporal_local * scale, spatial_local * scale), ('tm', 'height'...]
    all_to_all x1 -> x0, blocking collectives: 44.8 us -> none  [shards(): lax.all_to_all(arranged, ('tm', 'height'), split_axis=0, concat_axis=0, t...]
    pallas_call x0 -> x1, Pallas kernels: none -> 36.1 us  [all_reduce(): pl.pallas_call(functools.partial(reduce_kernel, n_tm, n_h), out_shape=jax...]
    all_to_all x1 -> x3, starting transfers between devices: 12.8 us -> 25.7 us  [the longest x1 9.9 us: shards(): lax.all_to_all(frame_total.astype(jnp.bfloat16), 'height', split_axis=0,...]
    ppermute x8, starting transfers between devices: 18.6 us -> 30.9 us  [the longest x4 19.1 us: joined(): after = lax.ppermute(head, axis, list(zip(order[1:], order[:-1])))]
    all_to_all x1 -> x3, waiting for transfers between devices: 21 us -> 15.2 us  [the longest x1 15.2 us: shards(): lax.all_to_all(bands, 'height', split_axis=0, concat_axis=0, tiled=True)]
    mul x3 -> x7, local copies, waits for them, and re-layouts: 0.25 us -> 5.59 us  [shards(): padded[:, 2 - lag:2 - lag + frames] * masks[lag][None, :, None, None]]
    dot_general x9, matrix products: 4.38 us -> 9.44 us  [shards(): jnp.dot(piece, spatial_weight[row_off, col_off], preferred_element_type=j...]
  transfers between devices with their start and end apart: 10 -> 11, of which waited for: 7 -> 5; matrix products, arithmetic and copies ran while one was open for 3% -> 16% of each run, Pallas kernels for 0% -> 20%
where the time goes in v1:
time: 182 us; the launch traced here: 181 us
  starting transfers between devices  56.6 us (31%)
  Pallas kernels  36.1 us (20%)
  waiting for transfers between devices  27.6 us (15%)
  matrix products  26.1 us (14%)
  local copies, waits for them, and re-layouts  23.2 us (13%)
  other arithmetic  10.1 us (6%)
    pallas_call x1, Pallas kernels, all_reduce(): pl.pallas_call(functools.partial(reduce_kernel, n_tm, n_h), out_shape=jax...  36.1 us
    ppermute x4, starting transfers between devices, joined(): after = lax.ppermute(head, axis, list(zip(order[1:], order[:-1])))  19.1 us
    all_to_all x1, waiting for transfers between devices, shards(): lax.all_to_all(bands, 'height', split_axis=0, concat_axis=0, tiled=True)  15.2 us
    ppermute x4, starting transfers between devices, joined(): before = lax.ppermute(tail, axis, list(zip(order[:-1], order[1:])))  11.8 us
    all_to_all x1, starting transfers between devices, shards(): lax.all_to_all(frame_total.astype(jnp.bfloat16), 'height', split_axis=0,...  9.9 us
    dot_general x9, matrix products, shards(): jnp.dot(piece, spatial_weight[row_off, col_off], preferred_element_type=j...  9.44 us
    ppermute x4, waiting for transfers between devices, joined(): before = lax.ppermute(tail, axis, list(zip(order[:-1], order[1:])))  8.6 us
    all_to_all x1, starting transfers between devices, shards(): lax.all_to_all(out_grad[0], 'tm', split_axis=0, concat_axis=0, tiled=True)  8.19 us
  transfers between devices with their start and end apart: 11, of which 5 were waited for; matrix products, arithmetic and copies ran while one was open for 16% of the time, Pallas kernels for 20%

profile of v1, /device:TPU:1, one launch (start us, length us, event | category | flops | bytes accessed | tf_op | source)
XLA Modules:
  0.0 180.9 jit_solution(17767011993468112196)
XLA Ops:
  0.6 2.5 %copy.20 = bf16[16,16,16,128]{3,2,1,0:T(8,128)(2,1)} copy(bf16[16,16,16,128]{3,2,0,1:T(8,128)(2,1)} %bitcast.218) | data formatting | bytes 2097152 | tf_op jit(solution)/shard_map/transpose | solution.py:172
  3.1 7.6 %all-to-all-start.1 = ((bf16[16,16,16,128]{3,2,1,0:T(8,128)(2,1)}), bf16[16,16,16,128]{3,2,1,0:T(8,128)(2,1)S(1)}, u32[]{:S(2)}, u32[]{:S(2)}) async-start(bf16[16,16,16,128]{3,2,1,0:T(8,128)(2,1)} %copy.20), calls=%async_computation.1 | async-start | bytes 2097152 | tf_op jit(solution)/shard_map/all_to_all | solution.py:173
  11.0 15.2 %all-to-all-done.1 = bf16[16,16,16,128]{3,2,1,0:T(8,128)(2,1)S(1)} async-done(((bf16[16,16,16,128]{3,2,1,0:T(8,128)(2,1)}), bf16[16,16,16,128]{3,2,1,0:T(8,128)(2,1)S(1)}, u32[]{:S(2)}, u32[]{:S(2)}) %all-to-all-start.1) | async-done | bytes 1048608 | tf_op jit(solution)/shard_map/all_to_all | solution.py:173
  26.5 0.6 copy-done.21
  28.0 0.4 fusion.2
  28.4 0.9 fusion.69
  29.3 2.2 %collective-permute-start = (bf16[16,16,1,128]{3,2,1,0:T(2,128)(2,1)}, bf16[16,16,1,128]{3,2,1,0:T(2,128)(2,1)S(1)}, u32[]{:S(2)}, u32[]{:S(2)}) collective-permute-start(bf16[16,16,1,128]{3,2,1,0:T(2,128)(2,1)} %get-tuple-element.32), channel_id=1, source_target_pairs={{0,2},{2,4},{4,6},{6,8},{8,10},{10,12},{12,14},{14,16},{16,18},{18... | collective-permute-start | bytes 196616 | tf_op jit(solution)/shard_map/ppermute | solution.py:134
  31.5 1.3 collective-permute-start.1
  32.8 8.2 %all-to-all-start = ((bf16[128,2,16,128]{3,2,1,0:T(8,128)(2,1)}), bf16[128,2,16,128]{3,2,1,0:T(8,128)(2,1)}, u32[]{:S(2)}, u32[]{:S(2)}) async-start(bf16[128,2,16,128]{3,2,1,0:T(8,128)(2,1)} %bitcast.219), calls=%async_computation | async-start | bytes 2097152 | tf_op jit(solution)/shard_map/all_to_all | solution.py:174
  41.0 0.7 mul.100
  41.7 0.9 mul.101
  42.7 0.7 mul.104
  43.4 0.9 mul.105
  44.3 0.7 mul.96
  45.0 1.6 mul.97
  46.7 3.4 %collective-permute-start.2 = (bf16[1,16,18,128]{3,2,1,0:T(8,128)(2,1)S(1)}, bf16[1,16,18,128]{3,2,1,0:T(8,128)(2,1)S(1)}, u32[]{:S(2)}, u32[]{:S(2)}) collective-permute-start(bf16[1,16,18,128]{3,2,1,0:T(8,128)(2,1)S(1)} %get-tuple-element.21), channel_id=1, source_target_pairs={{0,32},{32,64},{64,96},{96,128},{128,160},{160,192},{192,224},{224... | collective-permute-start | bytes 221192 | tf_op jit(solution)/shard_map/ppermute | solution.py:134
  50.1 7.2 %collective-permute-start.3 = (bf16[1,16,18,128]{3,2,1,0:T(8,128)(2,1)S(1)}, bf16[1,16,18,128]{3,2,1,0:T(8,128)(2,1)S(1)}, u32[]{:S(2)}, u32[]{:S(2)}) collective-permute-start(bf16[1,16,18,128]{3,2,1,0:T(8,128)(2,1)S(1)} %get-tuple-element.22), channel_id=1, source_target_pairs={{32,0},{64,32},{96,64},{128,96},{160,128},{192,160},{224,192},{1,2... | collective-permute-start | bytes 221192 | tf_op jit(solution)/shard_map/ppermute | solution.py:135
  57.3 2.1 %pad_maximum_fusion.4 = (bf16[16,16,16,128]{3,2,1,0:T(8,128)(2,1)}, bf16[16,16,16,128]{3,2,1,0:T(8,128)(2,1)S(1)}) fusion(bf16[16,16,1,128]{3,2,1,0:T(2,128)(2,1)S(1)} %collective-permute-done.1, bf16[16,16,16,128]{3,2,1,0:T(8,128)(2,1)S(1)} %bitcast.183, bf16[16,16,1,128]{3,2,1,0:T(2,128)(2,1)S(1)} %collective-permute-done), kind=kLoop, calls=%fused_computation.46 | loop fusion | flops 4194304 | bytes 3276800 | tf_op jit(solution)/shard_map/concatenate | solution.py:136
  59.8 5.1 %collective-permute-done.2 = bf16[1,16,18,128]{3,2,1,0:T(8,128)(2,1)S(1)} collective-permute-done((bf16[1,16,18,128]{3,2,1,0:T(8,128)(2,1)S(1)}, bf16[1,16,18,128]{3,2,1,0:T(8,128)(2,1)S(1)}, u32[]{:S(2)}, u32[]{:S(2)}) %collective-permute-start.2) | collective-permute-done | bytes 73760 | tf_op jit(solution)/shard_map/ppermute | solution.py:134
  64.9 2.0 %maximum_maximum_fusion = (bf16[17,16,18,128]{3,2,1,0:T(8,128)(2,1)S(1)}, bf16[17,16,18,128]{3,2,1,0:T(8,128)(2,1)S(1)}) fusion(bf16[16,16,1,128]{3,2,1,0:T(2,128)(2,1)S(1)} %collective-permute-done.1, bf16[16,16,16,128]{3,2,1,0:T(8,128)(2,1)S(1)} %bitcast.184, bf16[16,16,1,128]{3,2,1,0:T(2,128)(2,1)S(1)} %collective-permute-done, ...), kind=kLoop, calls=%fused_computation.24 | loop fusion | flops 10027008 | bytes 3833856 | tf_op jit(solution)/shard_map/concatenate | solution.py:136
  66.9 1.4 fusion.66
  68.8 0.5 copy-done
  69.3 2.3 %fusion.15 = f32[4096,128]{1,0:T(8,128)} fusion(bf16[4096,128]{1,0:T(8,128)(2,1)S(1)} %bitcast.189, bf16[3,3,128,128]{3,2,1,0:T(8,128)(2,1)S(1)} %copy-done.18), kind=kOutput, calls=%fused_computation.66 | convolution fusion | flops 134217728 | bytes 3178496 | tf_op jit(solution)/shard_map/dot_general | solution.py:189
  73.3 1.8 convolution_add_fusion.8
  75.1 1.7 copy.19
  76.8 0.5 copy-done.17
  77.3 2.9 %fusion.5 = bf16[4096,128]{1,0:T(8,128)(2,1)S(1)} fusion(f32[8,16,2,16,128]{4,3,2,0,1:T(8,128)S(1)} %copy.19, f32[4096,128]{1,0:T(8,128)S(1)} %copy-done.17, f32[4096,128]{1,0:T(8,128)} %convolution_add_fusion.8, bf16[4096,128]{1,0:T(8,128)(2,1)S(1)} %bitcast.206, bf16[3,3,128,128]{3,2,1,0:T(8,128)(2,1)S(1)} %copy-done.19), kind=kOutput, calls=%fused_computation.22 | convolution fusion | flops 139984896 | bytes 8421376 | tf_op jit(solution)/shard_map/dot_general | solution.py:189
  80.3 0.5 convolution_dynamic-update-slice_fusion.11
  80.8 0.7 copy-done.13
  81.5 0.5 convolution_dynamic-update-slice_fusion.10
  82.0 0.5 convolution_dynamic-update-slice_fusion.9
  82.8 0.5 convolution_dynamic-update-slice_fusion.8
  83.3 0.5 convolution_dynamic-update-slice_fusion.7
  84.0 0.5 convolution_dynamic-update-slice_fusion.6
  84.6 0.5 convolution_dynamic-update-slice_fusion.5
  85.1 0.5 convolution_dynamic-update-slice_fusion.4
  85.8 4.2 %collective-permute-start.4 = (bf16[16,16,1,128]{3,2,1,0:T(2,128)(2,1)S(1)}, bf16[16,16,1,128]{3,2,1,0:T(2,128)(2,1)S(1)}, u32[]{:S(2)}, u32[]{:S(2)}) collective-permute-start(bf16[16,16,1,128]{3,2,1,0:T(2,128)(2,1)S(1)} %get-tuple-element.28), channel_id=1, source_target_pairs={{0,2},{2,4},{4,6},{6,8},{8,10},{10,12},{12,14},{14,16},{16,18},{18... | collective-permute-start | bytes 196616 | tf_op jit(solution)/shard_map/ppermute | solution.py:134
  90.0 1.3 collective-permute-start.5
  91.3 0.5 convolution_dynamic-update-slice_fusion.3
  91.9 3.8 %collective-permute-done.5 = bf16[16,16,1,128]{3,2,1,0:T(2,128)(2,1)S(1)} collective-permute-done((bf16[16,16,1,128]{3,2,1,0:T(2,128)(2,1)S(1)}, bf16[16,16,1,128]{3,2,1,0:T(2,128)(2,1)S(1)}, u32[]{:S(2)}, u32[]{:S(2)}) %collective-permute-start.5) | collective-permute-done | bytes 65568 | tf_op jit(solution)/shard_map/ppermute | solution.py:135
  95.8 9.3 %collective-permute-start.6 = (bf16[1,16,18,128]{3,2,1,0:T(8,128)(2,1)S(1)}, bf16[1,16,18,128]{3,2,1,0:T(8,128)(2,1)S(1)}, u32[]{:S(2)}, u32[]{:S(2)}) collective-permute-start(bf16[1,16,18,128]{3,2,1,0:T(8,128)(2,1)S(1)} %get-tuple-element.17), channel_id=1, source_target_pairs={{32,0},{64,32},{96,64},{128,96},{160,128},{192,160},{224,192},{1,2... | collective-permute-start | bytes 221192 | tf_op jit(solution)/shard_map/ppermute | solution.py:135
  105.1 2.1 %collective-permute-start.7 = (bf16[1,16,18,128]{3,2,1,0:T(8,128)(2,1)S(1)}, bf16[1,16,18,128]{3,2,1,0:T(8,128)(2,1)S(1)}, u32[]{:S(2)}, u32[]{:S(2)}) collective-permute-start(bf16[1,16,18,128]{3,2,1,0:T(8,128)(2,1)S(1)} %get-tuple-element.18), channel_id=1, source_target_pairs={{0,32},{32,64},{64,96},{96,128},{128,160},{160,192},{192,224},{224... | collective-permute-start | bytes 221192 | tf_op jit(solution)/shard_map/ppermute | solution.py:134
  107.2 1.1 pad_maximum_fusion.2
  108.8 3.4 %collective-permute-done.7 = bf16[1,16,18,128]{3,2,1,0:T(8,128)(2,1)S(1)} collective-permute-done((bf16[1,16,18,128]{3,2,1,0:T(8,128)(2,1)S(1)}, bf16[1,16,18,128]{3,2,1,0:T(8,128)(2,1)S(1)}, u32[]{:S(2)}, u32[]{:S(2)}) %collective-permute-start.7) | collective-permute-done | bytes 73760 | tf_op jit(solution)/shard_map/ppermute | solution.py:134
  112.2 2.0 %pad_maximum_fusion.1 = (bf16[17,16,18,128]{3,2,1,0:T(8,128)(2,1)S(1)}, bf16[17,16,18,128]{3,2,1,0:T(8,128)(2,1)S(1)}) fusion(bf16[1,16,18,128]{3,2,1,0:T(8,128)(2,1)S(1)} %collective-permute-done.6, bf16[16,16,1,128]{3,2,1,0:T(2,128)(2,1)S(1)} %collective-permute-done.5, bf16[16,16,16,128]{3,2,1,0:T(8,128)(2,1)S(1)} %bitcast.180, ...), kind=kLoop, calls=%fused_computation.26 | loop fusion | flops 10027008 | bytes 3833856 | tf_op jit(solution)/shard_map/concatenate | solution.py:136
  114.3 0.8 fusion.64
  115.1 0.8 fusion.65
  115.9 0.4 convolution_add_fusion.6
  116.3 0.4 convolution_add_fusion.5
  116.8 0.4 convolution_add_fusion.4
  117.7 0.4 fusion.13
  118.1 0.4 convolution_add_fusion.2
  118.5 0.4 convolution_add_fusion.1
  119.2 2.0 %broadcast_multiply_fusion.2 = (bf16[4096,128]{1,0:T(8,128)(2,1)S(1)}, bf16[4096,128]{1,0:T(8,128)(2,1)S(1)}, bf16[4096,128]{1,0:T(8,128)(2,1)S(1)}, bf16[4096,128]{1,0:T(8,128)(2,1)S(1)}) fusion(bf16[4096]{0:T(1024)(128)(2,1)S(1)} %copy-done.22, bf16[4096]{0:T(1024)(128)(2,1)S(1)} %mul.105, bf16[4096]{0:T(1024)(128)(2,1)S(1)} %mul.101, ...), kind=kOutput, calls=%fused_computation.50 | convolution fusion | flops 137363456 | bytes 9494528 | tf_op jit(solution)/shard_map/dot_general | solution.py:199
  122.1 1.4 add_convert_fusion
  123.5 9.9 %all-to-all-start.2 = ((bf16[16,16,16,128]{3,2,1,0:T(8,128)(2,1)}), bf16[16,16,16,128]{3,2,1,0:T(8,128)(2,1)}, u32[]{:S(2)}, u32[]{:S(2)}) async-start(bf16[16,16,16,128]{3,2,1,0:T(8,128)(2,1)} %add_convert_fusion), calls=%async_computation.2 | async-start | bytes 2097152 | tf_op jit(solution)/shard_map/all_to_all | solution.py:220
  133.4 1.1 convolution_dynamic-update-slice_fusion.2
  134.5 1.1 convolution_dynamic-update-slice_fusion.1
  135.6 1.1 convolution_dynamic-update-slice_fusion
  136.7 2.1 %broadcast_multiply_fusion.4.x_ref = f32[1536,128]{1,0:T(8,128)} fusion(f32[1536,128]{1,0:T(8,128)} %convolution_dynamic-update-slice_fusion), kind=kLoop, calls=%fused_computation.52 | loop fusion | flops 196608 | bytes 1572864 | tf_op jit(solution)/shard_map/mul | solution.py:218
  138.8 36.1 %shard_map.76 = f32[1536,128]{1,0:T(8,128)} custom-call(f32[1536,128]{1,0:T(8,128)} %broadcast_multiply_fusion.4.x_ref), custom_call_target="tpu_custom_call" | custom-call | tf_op jit(solution)/shard_map/pallas_call | solution.py:114
  174.9 1.9 %slice.219 = f32[1152,128]{1,0:T(8,128)} slice(f32[1536,128]{1,0:T(8,128)} %shard_map.76), slice={[0:1152], [0:128]} | slice | bytes 1179648 | tf_op jit(solution)/shard_map/slice | solution.py:225
  176.8 1.6 slice.218
  178.4 2.5 %copy.21 = bf16[16,16,16,128]{3,2,1,0:T(8,128)(2,1)} copy(bf16[16,16,16,128]{3,2,0,1:T(8,128)(2,1)} %bitcast.54) | data formatting | bytes 2097152 | tf_op jit(solution)/shard_map/transpose | solution.py:221
  (73 shorter events, 7.1 us)
Async XLA Ops:
  0.6 10.1 %copy-start.23 = (s32[4]{0:T(128)S(1)}, s32[4]{0:T(128)}, u32[]{:S(2)}) copy-start(s32[4]{0:T(128)} %param.7) | copy-start | bytes 52
  3.1 23.1 %all-to-all-start.1 = ((bf16[16,16,16,128]{3,2,1,0:T(8,128)(2,1)}), bf16[16,16,16,128]{3,2,1,0:T(8,128)(2,1)S(1)}, u32[]{:S(2)}, u32[]{:S(2)}) async-start(bf16[16,16,16,128]{3,2,1,0:T(8,128)(2,1)} %copy.20), calls=%async_computation.1 | async-start | bytes 2097152 | tf_op jit(solution)/shard_map/all_to_all | solution.py:173
  26.2 0.9 copy-start.21
  26.5 1.4 copy-start.14
  29.3 17.3 %collective-permute-start = (bf16[16,16,1,128]{3,2,1,0:T(2,128)(2,1)}, bf16[16,16,1,128]{3,2,1,0:T(2,128)(2,1)S(1)}, u32[]{:S(2)}, u32[]{:S(2)}) collective-permute-start(bf16[16,16,1,128]{3,2,1,0:T(2,128)(2,1)} %get-tuple-element.32), channel_id=1, source_target_pairs={{0,2},{2,4},{4,6},{6,8},{8,10},{10,12},{12,14},{14,16},{16,18},{18... | collective-permute-start | bytes 196616 | tf_op jit(solution)/shard_map/ppermute | solution.py:134
  31.5 15.1 %collective-permute-start.1 = (bf16[16,16,1,128]{3,2,1,0:T(2,128)(2,1)}, bf16[16,16,1,128]{3,2,1,0:T(2,128)(2,1)S(1)}, u32[]{:S(2)}, u32[]{:S(2)}) collective-permute-start(bf16[16,16,1,128]{3,2,1,0:T(2,128)(2,1)} %get-tuple-element.33), channel_id=1, source_target_pairs={{2,0},{4,2},{6,4},{8,6},{10,8},{12,10},{14,12},{16,14},{18,16},{20... | collective-permute-start | bytes 196616 | tf_op jit(solution)/shard_map/ppermute | solution.py:135
  32.8 42.3 %all-to-all-start = ((bf16[128,2,16,128]{3,2,1,0:T(8,128)(2,1)}), bf16[128,2,16,128]{3,2,1,0:T(8,128)(2,1)}, u32[]{:S(2)}, u32[]{:S(2)}) async-start(bf16[128,2,16,128]{3,2,1,0:T(8,128)(2,1)} %bitcast.219), calls=%async_computation | async-start | bytes 2097152 | tf_op jit(solution)/shard_map/all_to_all | solution.py:174
  46.6 12.8 %copy-start.18 = (bf16[3,3,128,128]{3,2,1,0:T(8,128)(2,1)S(1)}, bf16[3,3,128,128]{3,2,1,0:T(8,128)(2,1)}, u32[]{:S(2)}) copy-start(bf16[3,3,128,128]{3,2,1,0:T(8,128)(2,1)} %param.9) | copy-start | bytes 884740
  46.7 18.1 %collective-permute-start.2 = (bf16[1,16,18,128]{3,2,1,0:T(8,128)(2,1)S(1)}, bf16[1,16,18,128]{3,2,1,0:T(8,128)(2,1)S(1)}, u32[]{:S(2)}, u32[]{:S(2)}) collective-permute-start(bf16[1,16,18,128]{3,2,1,0:T(8,128)(2,1)S(1)} %get-tuple-element.21), channel_id=1, source_target_pairs={{0,32},{32,64},{64,96},{96,128},{128,160},{160,192},{192,224},{224... | collective-permute-start | bytes 221192 | tf_op jit(solution)/shard_map/ppermute | solution.py:134
  50.1 14.8 %collective-permute-start.3 = (bf16[1,16,18,128]{3,2,1,0:T(8,128)(2,1)S(1)}, bf16[1,16,18,128]{3,2,1,0:T(8,128)(2,1)S(1)}, u32[]{:S(2)}, u32[]{:S(2)}) collective-permute-start(bf16[1,16,18,128]{3,2,1,0:T(8,128)(2,1)S(1)} %get-tuple-element.22), channel_id=1, source_target_pairs={{32,0},{64,32},{96,64},{128,96},{160,128},{192,160},{224,192},{1,2... | collective-permute-start | bytes 221192 | tf_op jit(solution)/shard_map/ppermute | solution.py:135
  59.4 7.5 %copy-start.12 = (bf16[16,16,16,128]{3,2,1,0:T(8,128)(2,1)}, bf16[16,16,16,128]{3,2,1,0:T(8,128)(2,1)S(1)}, u32[]{:S(2)}) copy-start(bf16[16,16,16,128]{3,2,1,0:T(8,128)(2,1)S(1)} %get-tuple-element.31) | copy-start | bytes 3145732
  68.3 1.0 copy-start
  68.3 3.3 %copy-start.8 = (bf16[16,16,16,128]{3,2,1,0:T(8,128)(2,1)}, bf16[16,16,16,128]{3,2,1,0:T(8,128)(2,1)S(1)}, u32[]{:S(2)}) copy-start(bf16[16,16,16,128]{3,2,1,0:T(8,128)(2,1)S(1)} %get-tuple-element.44) | copy-start | bytes 3145732
  68.4 3.7 %copy-start.10 = (bf16[16,16,16,128]{3,2,1,0:T(8,128)(2,1)}, bf16[16,16,16,128]{3,2,1,0:T(8,128)(2,1)S(1)}, u32[]{:S(2)}) copy-start(bf16[16,16,16,128]{3,2,1,0:T(8,128)(2,1)S(1)} %get-tuple-element.11) | copy-start | bytes 3145732
  68.4 3.7 %copy-start.6 = (bf16[16,16,16,128]{3,2,1,0:T(8,128)(2,1)}, bf16[16,16,16,128]{3,2,1,0:T(8,128)(2,1)S(1)}, u32[]{:S(2)}) copy-start(bf16[16,16,16,128]{3,2,1,0:T(8,128)(2,1)S(1)} %get-tuple-element.10) | copy-start | bytes 3145732
  68.4 4.5 %copy-start.4 = (bf16[16,16,16,128]{3,2,1,0:T(8,128)(2,1)}, bf16[16,16,16,128]{3,2,1,0:T(8,128)(2,1)S(1)}, u32[]{:S(2)}) copy-start(bf16[16,16,16,128]{3,2,1,0:T(8,128)(2,1)S(1)} %get-tuple-element.46) | copy-start | bytes 3145732
  68.4 4.9 %copy-start.2 = (bf16[16,16,16,128]{3,2,1,0:T(8,128)(2,1)}, bf16[16,16,16,128]{3,2,1,0:T(8,128)(2,1)S(1)}, u32[]{:S(2)}) copy-start(bf16[16,16,16,128]{3,2,1,0:T(8,128)(2,1)S(1)} %get-tuple-element.9) | copy-start | bytes 3145732
  73.3 3.4 %copy-start.19 = (bf16[3,3,128,128]{3,2,1,0:T(8,128)(2,1)S(1)}, bf16[3,3,128,128]{3,2,1,0:T(8,128)(2,1)}, u32[]{:S(2)}) copy-start(bf16[3,3,128,128]{3,2,1,0:T(8,128)(2,1)} %param.9) | copy-start | bytes 884740
  75.1 1.7 copy-start.16
  75.1 2.2 %copy-start.17 = (f32[4096,128]{1,0:T(8,128)S(1)}, f32[4096,128]{1,0:T(8,128)}, u32[]{:S(2)}) copy-start(f32[4096,128]{1,0:T(8,128)} %fusion.15) | copy-start | bytes 6291460
  77.3 2.9 %copy-start.11 = (bf16[16,16,16,128]{3,2,1,0:T(8,128)(2,1)S(1)}, bf16[16,16,16,128]{3,2,1,0:T(8,128)(2,1)}, u32[]{:S(2)}) copy-start(bf16[16,16,16,128]{3,2,1,0:T(8,128)(2,1)} %copy-done.10) | copy-start | bytes 3145732
  80.3 1.2 copy-start.13
  80.3 1.7 copy-start.9
  81.5 1.3 copy-start.7
  82.8 1.2 copy-start.5
  83.3 1.3 copy-start.3
  84.6 6.7 %copy-start.1 = (bf16[16,16,16,128]{3,2,1,0:T(8,128)(2,1)S(1)}, bf16[16,16,16,128]{3,2,1,0:T(8,128)(2,1)}, u32[]{:S(2)}) copy-start(bf16[16,16,16,128]{3,2,1,0:T(8,128)(2,1)} %copy-done) | copy-start | bytes 3145732
  85.8 6.1 %collective-permute-start.4 = (bf16[16,16,1,128]{3,2,1,0:T(2,128)(2,1)S(1)}, bf16[16,16,1,128]{3,2,1,0:T(2,128)(2,1)S(1)}, u32[]{:S(2)}, u32[]{:S(2)}) collective-permute-start(bf16[16,16,1,128]{3,2,1,0:T(2,128)(2,1)S(1)} %get-tuple-element.28), channel_id=1, source_target_pairs={{0,2},{2,4},{4,6},{6,8},{8,10},{10,12},{12,14},{14,16},{16,18},{18... | collective-permute-start | bytes 196616 | tf_op jit(solution)/shard_map/ppermute | solution.py:134
  90.0 5.7 %collective-permute-start.5 = (bf16[16,16,1,128]{3,2,1,0:T(2,128)(2,1)S(1)}, bf16[16,16,1,128]{3,2,1,0:T(2,128)(2,1)S(1)}, u32[]{:S(2)}, u32[]{:S(2)}) collective-permute-start(bf16[16,16,1,128]{3,2,1,0:T(2,128)(2,1)S(1)} %get-tuple-element.29), channel_id=1, source_target_pairs={{2,0},{4,2},{6,4},{8,6},{10,8},{12,10},{14,12},{16,14},{18,16},{20... | collective-permute-start | bytes 196616 | tf_op jit(solution)/shard_map/ppermute | solution.py:135
  91.8 16.6 %copy-start.20 = (f32[1536,128]{1,0:T(8,128)}, f32[1536,128]{1,0:T(8,128)S(1)}, u32[]{:S(2)}) copy-start(f32[1536,128]{1,0:T(8,128)S(1)} %convolution_dynamic-update-slice_fusion.3) | copy-start | bytes 2359300
  95.8 13.0 %collective-permute-start.6 = (bf16[1,16,18,128]{3,2,1,0:T(8,128)(2,1)S(1)}, bf16[1,16,18,128]{3,2,1,0:T(8,128)(2,1)S(1)}, u32[]{:S(2)}, u32[]{:S(2)}) collective-permute-start(bf16[1,16,18,128]{3,2,1,0:T(8,128)(2,1)S(1)} %get-tuple-element.17), channel_id=1, source_target_pairs={{32,0},{64,32},{96,64},{128,96},{160,128},{192,160},{224,192},{1,2... | collective-permute-start | bytes 221192 | tf_op jit(solution)/shard_map/ppermute | solution.py:135
  105.1 7.1 %collective-permute-start.7 = (bf16[1,16,18,128]{3,2,1,0:T(8,128)(2,1)S(1)}, bf16[1,16,18,128]{3,2,1,0:T(8,128)(2,1)S(1)}, u32[]{:S(2)}, u32[]{:S(2)}) collective-permute-start(bf16[1,16,18,128]{3,2,1,0:T(8,128)(2,1)S(1)} %get-tuple-element.18), channel_id=1, source_target_pairs={{0,32},{32,64},{64,96},{96,128},{128,160},{160,192},{192,224},{224... | collective-permute-start | bytes 221192 | tf_op jit(solution)/shard_map/ppermute | solution.py:134
  118.5 0.7 copy-start.22
  123.5 54.9 %all-to-all-start.2 = ((bf16[16,16,16,128]{3,2,1,0:T(8,128)(2,1)}), bf16[16,16,16,128]{3,2,1,0:T(8,128)(2,1)}, u32[]{:S(2)}, u32[]{:S(2)}) async-start(bf16[16,16,16,128]{3,2,1,0:T(8,128)(2,1)} %add_convert_fusion), calls=%async_computation.2 | async-start | bytes 2097152 | tf_op jit(solution)/shard_map/all_to_all | solution.py:220
  133.4 2.2 %copy-start.15 = (bf16[16,16,16,128]{3,2,1,0:T(8,128)(2,1)S(1)}, bf16[16,16,16,128]{3,2,1,0:T(8,128)(2,1)}, u32[]{:S(2)}) copy-start(bf16[16,16,16,128]{3,2,1,0:T(8,128)(2,1)} %copy-done.14) | copy-start | bytes 3145732

commit v2 on v1

v2 whole, which is shorter than its diff:
```python
import functools

import jax
import jax.numpy as jnp
from jax import lax
from jax.experimental import pallas as pl
from jax.experimental.pallas import tpu as pltpu
from jax.sharding import PartitionSpec as P

MESH = pl.DeviceIdType.MESH
BF16 = jnp.bfloat16
F32 = jnp.float32


def started(copy):
    def body(d, carry):
        copy(d).start()
        return carry

    return body


def waited(copy):
    def body(d, carry):
        copy(d).wait()
        return carry

    return body


def kernel(
    n_tm, n_h, n_w, scale,
    video, out_grad, lengths, t_weight, s_weight,
    video_grad, sums,
    clip, grads, act, act_cols, act_rows, act_edge, delta, delta_cols, delta_rows, delta_edge,
    slope, act_grad, moved, plane, wide, s_total, terms, half, pair_buf, h_buf, z_buf,
    t_fwd, t_bwd, s_fwd, s_bwd,
    local_sem, vz_send, vz_recv, vh_send, vh_recv, a_send, a_recv, d_send, d_recv, o_send, o_recv,
    pair_sem, h_send, h_recv, z_send, z_recv, g_send, g_recv, f_send, f_recv,
):
    tm = lax.axis_index("tm")
    h = lax.axis_index("height")
    w = lax.axis_index("width")
    frames, cols, rows, chans = delta.shape
    pair = frames // n_tm
    up, down = (h + n_h - 1) % n_h, (h + 1) % n_h
    block = w * n_tm + tm
    blocks = n_w * n_tm
    left, right = (block + blocks - 1) % blocks, (block + 1) % blocks
    left_tm, left_w = left % n_tm, left // n_tm
    right_tm, right_w = right % n_tm, right // n_tm
    around = (
        (tm, up, w), (tm, down, w),
        (left_tm, h, left_w), (left_tm, up, left_w), (left_tm, down, left_w),
        (right_tm, h, right_w), (right_tm, up, right_w), (right_tm, down, right_w),
    )

    barrier = pltpu.get_barrier_semaphore()

    def greet_h(d, carry):
        pl.semaphore_signal(barrier, inc=1, device_id=(tm, (h + d) % n_h, w), device_id_type=MESH)
        return carry

    def greet_z(d, carry):
        pl.semaphore_signal(barrier, inc=1, device_id=((tm + d) % n_tm, h, w), device_id_type=MESH)
        return carry

    lax.fori_loop(1, n_tm, greet_z, 0)
    lax.fori_loop(1, n_h, greet_h, 0)
    pl.semaphore_signal(barrier, inc=1, device_id=(tm, h, 1 - w), device_id_type=MESH)
    for other in around[2:]:
        pl.semaphore_signal(barrier, inc=1, device_id=other, device_id_type=MESH)
    pl.semaphore_wait(barrier, n_tm - 1 + n_h - 1 + 1 + 6)

    def vz_copy(d):
        to = (tm + d) % n_tm
        return pltpu.make_async_remote_copy(
            src_ref=out_grad.at[0, pl.ds(to * cols, cols)], dst_ref=grads.at[tm],
            send_sem=vz_send.at[d], recv_sem=vz_recv.at[d], device_id=(to, h, w), device_id_type=MESH)

    def vh_copy(d):
        to = (h + d) % n_h
        return pltpu.make_async_remote_copy(
            src_ref=video.at[0, 0, :, pl.ds(pl.multiple_of(to * rows, rows), rows)], dst_ref=clip.at[pl.ds(2, frames), h],
            send_sem=vh_send.at[d], recv_sem=vh_recv.at[d], device_id=(tm, to, w), device_id_type=MESH)

    def step_of(j):
        return (((j + 1) // 2) * (2 * (j % 2) - 1) + n_tm) % n_tm

    lax.fori_loop(1, n_tm, lambda j, carry: started(vz_copy)(step_of(j), carry), 0)
    lax.fori_loop(1, n_h, started(vh_copy), 0)
    own_grad = pltpu.make_async_copy(out_grad.at[0, pl.ds(tm * cols, cols)], grads.at[tm], local_sem.at[0])
    own_clip = pltpu.make_async_copy(
        video.at[0, 0, :, pl.ds(pl.multiple_of(h * rows, rows), rows)], clip.at[pl.ds(2, frames), h], local_sem.at[1])
    own_grad.start()
    own_clip.start()

    for f in range(2):
        clip[f] = jnp.zeros((cols, rows, chans), BF16)
        act_grad[frames + f] = jnp.zeros((cols * rows, chans), BF16)
    for k in range(3):
        t_fwd[k * chans : (k + 1) * chans, :] = t_weight[k]
        t_bwd[k * chans : (k + 1) * chans, :] = t_weight[k].T
    for b in range(3):
        for a in range(3):
            place = pl.ds((b * 3 + a) * chans, chans)
            s_fwd[place, :] = s_weight[a, b]
            s_bwd[place, :] = s_weight[a, b].T
    s_total[...] = jnp.zeros_like(s_total)
    starts = [lengths[0], lengths[0] + lengths[1], lengths[0] + lengths[1] + lengths[2]]

    def mask(f, lag):
        keep = jnp.where(f >= lag, 1, 0)
        for start in starts:
            keep = jnp.where((start > f - lag) & (start <= f), 0, keep)
        return jnp.broadcast_to(keep.astype(F32), (rows, chans)).astype(BF16)[None]

    own_clip.wait()
    lax.fori_loop(1, n_h, waited(vh_copy), 0)

    def edges_of(value, edge, f):
        plane[...] = value.astype(F32)
        edge[0, f] = plane[pl.ds(0, cols, stride=rows), :].astype(BF16)
        edge[1, f] = plane[pl.ds(rows - 1, cols, stride=rows), :].astype(BF16)

    def act_frame(f, carry):
        taps = [clip[f + 2], clip[f + 1] * mask(f, 1), clip[f] * mask(f, 2)]
        taps = jnp.concatenate([tap.reshape(cols * rows, chans) for tap in taps], axis=1)
        value = jnp.dot(taps, t_fwd[...], preferred_element_type=F32).astype(BF16)
        act[f, 1 : cols + 1, :, chans : 2 * chans] = value.reshape(cols, rows, chans)
        edges_of(value, act_edge, f)
        return carry

    lax.fori_loop(0, frames, act_frame, 0)

    def halo_copies(edge, first, last, got_rows, got_cols, span, send, recv):
        parts = (
            (edge.at[0, span], got_rows.at[1, span]), (edge.at[1, span], got_rows.at[0, span]),
            (first, got_cols.at[1, 1, span]), (first, got_cols.at[1, 2, span]), (first, got_cols.at[1, 0, span]),
            (last, got_cols.at[0, 1, span]), (last, got_cols.at[0, 2, span]), (last, got_cols.at[0, 0, span]),
        )
        return [
            pltpu.make_async_remote_copy(
                src_ref=src, dst_ref=dst, send_sem=send.at[i], recv_sem=recv.at[i], device_id=around[i], device_id_type=MESH)
            for i, (src, dst) in enumerate(parts)
        ]

    mid = pl.ds(chans, chans)
    act_halo = halo_copies(
        act_edge, act.at[:, 1, :, mid], act.at[:, cols, :, mid], act_rows, act_cols, pl.ds(0, frames), a_send, a_recv)
    for copy in act_halo:
        copy.start()

    row = lax.broadcasted_iota(jnp.int32, (rows, chans), 0)
    is_first, is_last = row == 0, row == rows - 1
    has_up, has_down = h > 0, h < n_h - 1
    has_side = (block > 0, block < blocks - 1)

    def kept(flag, value):
        return jnp.where(flag, value, jnp.zeros_like(value))

    def shifted(middle, above, below):
        before = jnp.where(is_first, jnp.broadcast_to(above, middle.shape), pltpu.roll(middle, 1, 0))
        after = jnp.where(is_last, jnp.broadcast_to(below, middle.shape), pltpu.roll(middle, rows - 1, 0))
        return before.astype(BF16), after.astype(BF16)

    def with_halo(f, middle_of, got_rows, got_cols, put):
        above = kept(has_up, got_rows[0, f].astype(F32))
        below = kept(has_down, got_rows[1, f].astype(F32))
        for c in range(cols):
            middle = middle_of(c)
            before, after = shifted(middle.astype(F32), above[c : c + 1], below[c : c + 1])
            put(c + 1, before, middle, after)
        for side, c in ((0, 0), (1, cols + 1)):
            middle = kept(has_side[side], got_cols[side, 1, f].astype(F32))
            above_side = kept(has_side[side] & has_up, got_cols[side, 0, f].astype(F32))[rows - 1 : rows]
            below_side = kept(has_side[side] & has_down, got_cols[side, 2, f].astype(F32))[0:1]
            before, after = shifted(middle, above_side, below_side)
            put(c, before, middle.astype(BF16), after)

    for copy in act_halo:
        copy.wait()

    def slope_frame(f, carry):
        def put(c, before, middle, after):
            act[f, c, :, 0:chans] = before
            if c == 0 or c == cols + 1:
                act[f, c, :, chans : 2 * chans] = middle
            act[f, c, :, 2 * chans : 3 * chans] = after

        with_halo(f, lambda c: act[f, c + 1, :, chans : 2 * chans], act_rows, act_cols, put)
        wide_act = jnp.concatenate([act[f, b : b + cols].reshape(cols * rows, 3 * chans) for b in range(3)], axis=1)
        pre = jnp.dot(wide_act, s_fwd[...], preferred_element_type=F32)
        sig = jax.nn.sigmoid(pre)
        slope[f] = sig * (1.0 + pre * (1.0 - sig))
        return carry

    lax.fori_loop(0, frames, slope_frame, 0)

    def delta_halo(t):
        span = pl.ds(t * pair, pair)
        return halo_copies(
            delta_edge, delta.at[span, 0], delta.at[span, cols - 1], delta_rows, delta_cols, span, d_send.at[t], d_recv.at[t])

    own_grad.wait()

    def delta_pair(j, carry):
        d = step_of(j)
        t = (tm + n_tm - d) % n_tm

        @pl.when(j > 0)
        def _():
            vz_copy(d).wait()

        for i in range(pair):
            f = t * pair + i
            value = (grads[t, :, i].reshape(cols * rows, chans).astype(F32) * slope[f]).astype(BF16)
            delta[f] = value.reshape(cols, rows, chans)
            edges_of(value, delta_edge, f)
        for copy in delta_halo(t):
            copy.start()
        span = pl.ds(t * pair, pair)
        here = delta[span].reshape(pair * cols * rows, chans)
        for b in range(3):
            source = act[span, b : b + cols].reshape(pair * cols * rows, 3 * chans)
            s_total[:, b * 3 * chans : (b + 1) * 3 * chans] += lax.dot_general(
                here, source, (((0,), (0,)), ((), ())), preferred_element_type=F32)
        return carry

    lax.fori_loop(0, n_tm, delta_pair, 0)

    def back_pair(j, carry):
        t = (tm + n_tm - step_of(j)) % n_tm
        for copy in delta_halo(t):
            copy.wait()

        def back_frame(f, carry):
            def put(c, before, middle, after):
                wide[c, :, 0:chans] = after
                wide[c, :, chans : 2 * chans] = middle
                wide[c, :, 2 * chans : 3 * chans] = before

            with_halo(f, lambda c: delta[f, c], delta_rows, delta_cols, put)
            wide_delta = jnp.concatenate(
                [wide[2 - b : 2 - b + cols].reshape(cols * rows, 3 * chans) for b in range(3)], axis=1)
            act_grad[f] = jnp.dot(wide_delta, s_bwd[...], preferred_element_type=F32).astype(BF16)
            return carry

        return lax.fori_loop(t * pair, t * pair + pair, back_frame, carry)

    lax.fori_loop(0, n_tm, back_pair, 0)

    def time_frame(f, t_total):
        parts = [
            act_grad[f].reshape(cols, rows, chans),
            act_grad[f + 1].reshape(cols, rows, chans) * mask(f + 1, 1),
            act_grad[f + 2].reshape(cols, rows, chans) * mask(f + 2, 2),
        ]
        parts = jnp.concatenate([part.reshape(cols * rows, chans) for part in parts], axis=1)
        value = jnp.dot(parts, t_bwd[...], preferred_element_type=F32).astype(BF16)
        moved[f] = value.reshape(cols, rows, chans)
        here = clip[f + 2].reshape(cols * rows, chans)
        return t_total + lax.dot_general(here, parts, (((0,), (0,)), ((), ())), preferred_element_type=F32)

    t_total = lax.fori_loop(0, frames, time_frame, jnp.zeros((chans, 3 * chans), F32))

    def out_copy(d):
        to = (h + d) % n_h
        return pltpu.make_async_remote_copy(
            src_ref=moved.at[:, to], dst_ref=video_grad.at[0, 0, :, pl.ds(pl.multiple_of(h * rows, rows), rows)],
            send_sem=o_send.at[d], recv_sem=o_recv.at[d], device_id=(tm, to, w), device_id_type=MESH)

    lax.fori_loop(1, n_h, started(out_copy), 0)
    own_out = pltpu.make_async_copy(
        moved.at[:, h], video_grad.at[0, 0, :, pl.ds(pl.multiple_of(h * rows, rows), rows)], local_sem.at[2])
    own_out.start()

    for a in range(3):
        for b in range(3):
            terms[pl.ds((a * 3 + b) * chans, chans), :] = (
                s_total[:, (b * 3 + a) * chans : (b * 3 + a + 1) * chans].T * scale)
    for k in range(3):
        terms[pl.ds((9 + k) * chans, chans), :] = t_total[:, k * chans : (k + 1) * chans] * scale

    half_rows = half.shape[0]
    piece = half_rows // n_h
    mine = pl.multiple_of(w * half_rows, half_rows)
    swap = pltpu.make_async_remote_copy(
        src_ref=terms.at[pl.ds(pl.multiple_of((1 - w) * half_rows, half_rows), half_rows)], dst_ref=pair_buf,
        send_sem=pair_sem.at[0], recv_sem=pair_sem.at[1], device_id=(tm, h, 1 - w), device_id_type=MESH)
    swap.start()
    swap.wait()
    half[...] = terms[pl.ds(mine, half_rows), :] + pair_buf[...]

    def h_copy(d):
        to = (h + d) % n_h
        return pltpu.make_async_remote_copy(
            src_ref=half.at[pl.ds(pl.multiple_of(to * piece, 8), piece)], dst_ref=h_buf.at[d],
            send_sem=h_send.at[d], recv_sem=h_recv.at[d], device_id=(tm, to, w), device_id_type=MESH)

    lax.fori_loop(1, n_h, started(h_copy), 0)
    lax.fori_loop(1, n_h, waited(h_copy), 0)
    total = half[pl.ds(pl.multiple_of(h * piece, 8), piece), :]
    for d in range(1, n_h):
        total = total + h_buf[d]
    z_buf[tm] = total

    def z_copy(d):
        return pltpu.make_async_remote_copy(
            src_ref=z_buf.at[tm], dst_ref=z_buf.at[tm],
            send_sem=z_send.at[d], recv_sem=z_recv.at[d], device_id=((tm + d) % n_tm, h, w), device_id_type=MESH)

    lax.fori_loop(1, n_tm, started(z_copy), 0)
    lax.fori_loop(1, n_tm, waited(z_copy), 0)
    total = z_buf[0]
    for t in range(1, n_tm):
        total = total + z_buf[t]
    here = pl.ds(pl.multiple_of(mine + h * piece, 8), piece)
    sums[here, :] = total

    def g_copy(d):
        return pltpu.make_async_remote_copy(
            src_ref=sums.at[here], dst_ref=sums.at[here],
            send_sem=g_send.at[d], recv_sem=g_recv.at[d], device_id=(tm, (h + d) % n_h, w), device_id_type=MESH)

    def f_copy(d):
        there = pl.ds(pl.multiple_of(mine + ((h + n_h - d) % n_h) * piece, 8), piece)
        return pltpu.make_async_remote_copy(
            src_ref=sums.at[there], dst_ref=sums.at[there],
            send_sem=f_send.at[d], recv_sem=f_recv.at[d], device_id=(tm, h, 1 - w), device_id_type=MESH)

    lax.fori_loop(1, n_h, started(g_copy), 0)
    f_copy(0).start()

    def forward(d, carry):
        g_copy(d).wait()
        f_copy(d).start()
        return carry

    lax.fori_loop(1, n_h, forward, 0)
    lax.fori_loop(0, n_h, waited(f_copy), 0)
    own_out.wait()
    lax.fori_loop(1, n_h, waited(out_copy), 0)


def shards(n_tm, n_h, n_w, video, out_grad, lengths, temporal_weight, spatial_weight):
    frames, all_rows, chans = video.shape[2:]
    rows = all_rows // n_h
    cols = out_grad.shape[1] // n_tm
    pair = frames // n_tm
    lags = temporal_weight.shape[0]
    offs = spatial_weight.shape[0]
    n_terms = (lags + offs * offs) * chans
    piece = n_terms // n_w // n_h
    scale = float(frames * all_rows * cols * n_tm * n_w) ** (-0.5)
    dma = pltpu.SemaphoreType.DMA
    vmem = pltpu.VMEM
    video_grad, sums = pl.pallas_call(
        functools.partial(kernel, n_tm, n_h, n_w, scale),
        out_shape=(jax.ShapeDtypeStruct(video.shape, BF16), jax.ShapeDtypeStruct((n_terms, chans), F32)),
        in_specs=[
            pl.BlockSpec(memory_space=pl.ANY),
            pl.BlockSpec(memory_space=pl.ANY),
            pl.BlockSpec(memory_space=pltpu.SMEM),
            pl.BlockSpec(memory_space=pltpu.VMEM),
            pl.BlockSpec(memory_space=pltpu.VMEM),
        ],
        out_specs=(pl.BlockSpec(memory_space=pl.ANY), pl.BlockSpec(memory_space=pltpu.VMEM)),
        scratch_shapes=[
            vmem((frames + 2, cols, rows, chans), BF16),
            vmem((n_tm, cols, pair, rows, chans), BF16),
            vmem((frames, cols + 2, rows, 3 * chans), BF16),
            vmem((2, 3, frames, rows, chans), BF16),
            vmem((2, frames, cols, chans), BF16),
            vmem((2, frames, cols, chans), BF16),
            vmem((frames, cols, rows, chans), BF16),
            vmem((2, 3, frames, rows, chans), BF16),
            vmem((2, frames, cols, chans), BF16),
            vmem((2, frames, cols, chans), BF16),
            vmem((frames, cols * rows, chans), F32),
            vmem((frames + 2, cols * rows, chans), BF16),
            vmem((frames, cols, rows, chans), BF16),
            vmem((cols * rows, chans), F32),
            vmem((cols + 2, rows, 3 * chans), BF16),
            vmem((chans, offs * offs * chans), F32),
            vmem((n_terms, chans), F32),
            vmem((n_terms // 2, chans), F32),
            vmem((n_terms // 2, chans), F32),
            vmem((n_h, piece, chans), F32),
            vmem((n_tm, piece, chans), F32),
            vmem((lags * chans, chans), BF16),
            vmem((lags * chans, chans), BF16),
            vmem((offs * offs * chans, chans), BF16),
            vmem((offs * offs * chans, chans), BF16),
            dma((3,)), dma((n_tm,)), dma((n_tm,)), dma((n_h,)), dma((n_h,)), dma((8,)), dma((8,)), dma((n_tm, 8)), dma((n_tm, 8)),
            dma((n_h,)), dma((n_h,)),
            dma((2,)), dma((n_h,)), dma((n_h,)), dma((n_tm,)), dma((n_tm,)), dma((n_h,)), dma((n_h,)), dma((n_h,)), dma((n_h,)),
        ],
        compiler_params=pltpu.CompilerParams(collective_id=0, has_side_effects=True, vmem_limit_bytes=48 << 20),
    )(video, out_grad, lengths, temporal_weight, spatial_weight)
    split = offs * offs * chans
    return (
        video_grad,
        sums[split:].reshape(lags, chans, chans),
        sums[:split].reshape(offs, offs, chans, chans),
    )


def solution(mesh):
    placed = (
        P("width", ("tm", "height"), None, None, None),
        P("width", None, "tm", "height", None),
        P(),
        P(),
        P(),
    )
    return jax.shard_map(
        functools.partial(shards, mesh.shape["tm"], mesh.shape["height"], mesh.shape["width"]),
        mesh=mesh,
        in_specs=placed,
        out_specs=(P("width", ("tm", "height"), None, None, None), P(), P()),
        check_vma=False,
    )
```

time: 182 us -> 111 us (0.61)
  Pallas kernels: 36.1 us -> 102 us
  starting transfers between devices: 56.6 us -> 0 us
  waiting for transfers between devices: 27.6 us -> 0 us
  matrix products: 26.1 us -> 0 us
  local copies, waits for them, and re-layouts: 23.2 us -> 7.46 us
  other arithmetic: 10.1 us -> 0 us
    pallas_call x1, Pallas kernels: 36.1 us -> 102 us  [shards(): pl.pallas_call(functools.partial(kernel, n_tm, n_h, n_w, scale), out_shap...]
    ppermute x8 -> x0, starting transfers between devices: 30.9 us -> none  [the longest x4 19.1 us: joined(): after = lax.ppermute(head, axis, list(zip(order[1:], order[:-1])))]
    all_to_all x3 -> x0, starting transfers between devices: 25.7 us -> none  [the longest x1 9.9 us: shards(): lax.all_to_all(frame_total.astype(jnp.bfloat16), 'height', split_axis=0,...]
    dot_general x34 -> x0, matrix products: 25.3 us -> none  [the longest x9 9.44 us: shards(): jnp.dot(piece, spatial_weight[row_off, col_off], preferred_element_type=j...]
    all_to_all x3 -> x0, waiting for transfers between devices: 15.2 us -> none  [the longest x1 15.2 us: shards(): lax.all_to_all(bands, 'height', split_axis=0, concat_axis=0, tiled=True)]
    ppermute x8 -> x0, waiting for transfers between devices: 12.4 us -> none  [the longest x4 8.6 us: joined(): before = lax.ppermute(tail, axis, list(zip(order[:-1], order[1:])))]
    concatenate x4 -> x0, other arithmetic: 7.24 us -> none  [joined(): return jnp.concatenate([before, cells, after], axis=dim)]
    slice x7 -> x2, local copies, waits for them, and re-layouts: 7.7 us -> 1.54 us  [the longest x1 0.85 us: shards(): sums[:split].reshape(offs, offs, chans, chans)]
  transfers between devices with their start and end apart: 11 -> 0, of which waited for: 5 -> 0; matrix products, arithmetic and copies ran while one was open for 16% -> 0% of each run, Pallas kernels for 20% -> 0%
where the time goes in v2:
time: 111 us; the launch traced here: 110 us
  Pallas kernels  102 us (92%)
  local copies, waits for them, and re-layouts  7.46 us (7%)
    pallas_call x1, Pallas kernels, shards(): pl.pallas_call(functools.partial(kernel, n_tm, n_h, n_w, scale), out_shap...  102 us
    unnamed x11, local copies, waits for them, and re-layouts  5.92 us

profile of v2, /device:TPU:1, one launch (start us, length us, event | category | flops | bytes accessed | tf_op | source)
XLA Modules:
  0.0 110.3 jit_solution(7410755300218109687)
XLA Ops:
  0.6 0.0 copy-start
  0.6 1.2 %copy-done = bf16[1,1,16,256,128]{4,3,2,1,0:T(8,128)(2,1)S(1)} copy-done((bf16[1,1,16,256,128]{4,3,2,1,0:T(8,128)(2,1)S(1)}, bf16[1,1,16,256,128]{4,3,2,1,0:T(8,128)(2,1)}, u32[]{:S(2)}) %copy-start) | copy-done | bytes 1048600
  1.9 0.0 copy-start.1
  1.9 1.2 %copy-done.1 = bf16[1,128,2,16,128]{4,3,2,1,0:T(8,128)(2,1)S(1)} copy-done((bf16[1,128,2,16,128]{4,3,2,1,0:T(8,128)(2,1)S(1)}, bf16[1,128,2,16,128]{4,3,2,1,0:T(8,128)(2,1)}, u32[]{:S(2)}) %copy-start.1) | copy-done | bytes 1048600
  3.1 0.0 copy-start.2
  3.1 1.0 copy-done.2
  4.0 0.0 copy-start.3
  4.0 0.9 copy-done.3
  4.9 0.0 copy-start.4
  4.9 0.7 copy-done.4
  5.6 102.2 %shard_map.76 = (bf16[1,1,16,256,128]{4,3,2,1,0:T(8,128)(2,1)S(1)}, f32[1536,128]{1,0:T(8,128)S(1)}) custom-call(bf16[1,1,16,256,128]{4,3,2,1,0:T(8,128)(2,1)S(1)} %copy-done, bf16[1,128,2,16,128]{4,3,2,1,0:T(8,128)(2,1)S(1)} %copy-done.1, s32[4]{0:T(128)S(1)} %copy-done.4, bf16[3,128,128]{2,1,0:T(8,128)(2,1)S(1)} %copy-done.3, ...), custom_call_target="tpu_custom_call" | custom-call | tf_op jit(solution)/shard_map/pallas_call | solution.py:358
  107.8 0.7 slice.6
  108.5 0.9 slice.7
  109.4 1.0 copy.9
Async XLA Ops:
  0.6 1.2 %copy-start = (bf16[1,1,16,256,128]{4,3,2,1,0:T(8,128)(2,1)S(1)}, bf16[1,1,16,256,128]{4,3,2,1,0:T(8,128)(2,1)}, u32[]{:S(2)}) copy-start(bf16[1,1,16,256,128]{4,3,2,1,0:T(8,128)(2,1)} %video.1) | copy-start | bytes 3145732
  1.9 1.2 %copy-start.1 = (bf16[1,128,2,16,128]{4,3,2,1,0:T(8,128)(2,1)S(1)}, bf16[1,128,2,16,128]{4,3,2,1,0:T(8,128)(2,1)}, u32[]{:S(2)}) copy-start(bf16[1,128,2,16,128]{4,3,2,1,0:T(8,128)(2,1)} %out_grad.1) | copy-start | bytes 3145732
  3.1 1.0 copy-start.2
  4.0 0.9 copy-start.3
  4.9 0.7 copy-start.4

commit v3 on v2

v3 whole, which is shorter than its diff:
```python
import functools

import jax
import jax.numpy as jnp
from jax import lax
from jax.experimental import pallas as pl
from jax.experimental.pallas import tpu as pltpu
from jax.sharding import PartitionSpec as P

MESH = pl.DeviceIdType.MESH
BF16 = jnp.bfloat16
F32 = jnp.float32


def started(copy):
    def body(d, carry):
        copy(d).start()
        return carry

    return body


def waited(copy):
    def body(d, carry):
        copy(d).wait()
        return carry

    return body


def kernel(
    n_tm, n_h, n_w, scale,
    video, out_grad, lengths_in, t_weight_in, s_weight_in,
    video_grad, t_out, s_out,
    clip, grads, act, act_got, act_sent, delta, delta_got, delta_sent,
    slope, act_grad, moved, plane, wide, s_total, t_total, s_bufs, t_bufs,
    t_fwd, t_bwd, s_fwd, s_bwd, lengths, t_weight, s_weight,
    local_sem, vz_send, vz_recv, vh_send, vh_recv, a_send, a_recv, d_send, d_recv, o_send, o_recv, s_sems, t_sems,
):
    tm = lax.axis_index("tm")
    h = lax.axis_index("height")
    w = lax.axis_index("width")
    frames, cols, rows, chans = delta.shape
    pair = frames // n_tm
    up, down = (h + n_h - 1) % n_h, (h + 1) % n_h
    block = w * n_tm + tm
    blocks = n_w * n_tm
    left, right = (block + blocks - 1) % blocks, (block + 1) % blocks
    left_tm, left_w = left % n_tm, left // n_tm
    right_tm, right_w = right % n_tm, right // n_tm
    around = (
        (tm, up, w), (tm, down, w), (left_tm, h, left_w), (right_tm, h, right_w),
        (left_tm, up, left_w), (left_tm, down, left_w), (right_tm, up, right_w), (right_tm, down, right_w),
    )

    loads = [
        pltpu.make_async_copy(src, dst, local_sem.at[i])
        for i, (src, dst) in enumerate(((t_weight_in, t_weight), (s_weight_in, s_weight), (lengths_in, lengths)))
    ]
    for load in loads:
        load.start()
    barrier = pltpu.get_barrier_semaphore()

    def greet_h(d, carry):
        pl.semaphore_signal(barrier, inc=1, device_id=(tm, (h + d) % n_h, w), device_id_type=MESH)
        return carry

    def greet_z(d, carry):
        pl.semaphore_signal(barrier, inc=1, device_id=((tm + d) % n_tm, h, w), device_id_type=MESH)
        return carry

    lax.fori_loop(1, n_tm, greet_z, 0)
    lax.fori_loop(1, n_h, greet_h, 0)
    pl.semaphore_signal(barrier, inc=1, device_id=(tm, h, 1 - w), device_id_type=MESH)
    for other in around[2:]:
        pl.semaphore_signal(barrier, inc=1, device_id=other, device_id_type=MESH)
    pl.semaphore_wait(barrier, n_tm - 1 + n_h - 1 + 1 + 6)

    def vz_copy(d):
        to = (tm + d) % n_tm
        return pltpu.make_async_remote_copy(
            src_ref=out_grad.at[0, pl.ds(to * cols, cols)], dst_ref=grads.at[tm],
            send_sem=vz_send.at[d], recv_sem=vz_recv.at[d], device_id=(to, h, w), device_id_type=MESH)

    def vh_copy(d):
        to = (h + d) % n_h
        return pltpu.make_async_remote_copy(
            src_ref=video.at[0, 0, :, pl.ds(pl.multiple_of(to * rows, rows), rows)], dst_ref=clip.at[h, pl.ds(2, frames)],
            send_sem=vh_send.at[d], recv_sem=vh_recv.at[d], device_id=(tm, to, w), device_id_type=MESH)

    def step_of(j):
        return (((j + 1) // 2) * (2 * (j % 2) - 1) + n_tm) % n_tm

    early = n_tm - 2
    lax.fori_loop(1, n_h, started(vh_copy), 0)
    lax.fori_loop(1, early, lambda j, carry: started(vz_copy)(step_of(j), carry), 0)
    own_grad = pltpu.make_async_copy(out_grad.at[0, pl.ds(tm * cols, cols)], grads.at[tm], local_sem.at[3])
    own_clip = pltpu.make_async_copy(
        video.at[0, 0, :, pl.ds(pl.multiple_of(h * rows, rows), rows)], clip.at[h, pl.ds(2, frames)], local_sem.at[4])
    own_grad.start()
    own_clip.start()

    for f in range(2):
        clip[:, f] = jnp.zeros((cols, rows, chans), BF16)
        act_grad[frames + f] = jnp.zeros((cols * rows, chans), BF16)
    for load in loads:
        load.wait()
    for k in range(3):
        t_fwd[k * chans : (k + 1) * chans, :] = t_weight[k]
        t_bwd[k * chans : (k + 1) * chans, :] = t_weight[k].T
    for b in range(3):
        for a in range(3):
            place = pl.ds((b * 3 + a) * chans, chans)
            s_fwd[place, :] = s_weight[a, b]
            s_bwd[place, :] = s_weight[a, b].T
    s_total[...] = jnp.zeros_like(s_total)
    t_total[...] = jnp.zeros_like(t_total)
    delta_sent[1][...] = jnp.zeros_like(delta_sent[1])
    starts = [lengths[0], lengths[0] + lengths[1], lengths[0] + lengths[1] + lengths[2]]

    def mask(f, lag):
        keep = jnp.where(f >= lag, 1, 0)
        for start in starts:
            keep = jnp.where((start > f - lag) & (start <= f), 0, keep)
        return jnp.broadcast_to(keep.astype(F32), (rows, chans)).astype(BF16)[None]

    own_clip.wait()
    lax.fori_loop(1, n_h, waited(vh_copy), 0)

    def edges_of(value, sent, corner_at, f, i):
        edge, corner = sent
        plane[i] = value.astype(F32)
        edge[0, f] = plane[i, pl.ds(0, cols, stride=rows), :].astype(BF16)
        edge[1, f] = plane[i, pl.ds(rows - 1, cols, stride=rows), :].astype(BF16)
        for k, place in enumerate((0, rows - 1, (cols - 1) * rows, cols * rows - 1)):
            corner[corner_at(k)] = plane[i, place : place + 1, :]

    def act_corner(f):
        return lambda k: (k, pl.ds(f, 1))

    def delta_corner(t, i):
        return lambda k: (k, t, pl.ds(i, 1))

    def flat(blocks):
        return [block.reshape(cols * rows, chans) for block in blocks]

    def act_pair(t, carry):
        lines = []
        for i in range(pair):
            f = t * pair + i
            lines.append(jnp.concatenate(flat([clip[:, f + 2], clip[:, f + 1] * mask(f, 1), clip[:, f] * mask(f, 2)]), axis=1))
        both = jnp.dot(jnp.concatenate(lines, axis=0), t_fwd[...], preferred_element_type=F32).astype(BF16)
        for i in range(pair):
            value = both[i * cols * rows : (i + 1) * cols * rows]
            act[t * pair + i, 1 : cols + 1, :, chans : 2 * chans] = value.reshape(cols, rows, chans)
            edges_of(value, act_sent, act_corner(t * pair + i), t * pair + i, i)
        return carry

    lax.fori_loop(0, n_tm, act_pair, 0)

    def halo_copies(sent, got, first, last, span, part, send, recv):
        (edge, corner), (got_rows, got_cols, got_corner) = sent, got
        parts = [
            (edge.at[0, span], got_rows.at[1, span]), (edge.at[1, span], got_rows.at[0, span]),
            (first, got_cols.at[1, span]), (last, got_cols.at[0, span]),
        ] + [(corner.at[(k, *part)], got_corner.at[(3 - k, *part)]) for k in range(4)]
        return [
            pltpu.make_async_remote_copy(
                src_ref=src, dst_ref=dst, send_sem=send.at[i], recv_sem=recv.at[i], device_id=around[i], device_id_type=MESH)
            for i, (src, dst) in enumerate(parts)
        ]

    mid = pl.ds(chans, chans)
    act_halo = halo_copies(
        act_sent, act_got, act.at[:, 1, :, mid], act.at[:, cols, :, mid], pl.ds(0, frames), (), a_send, a_recv)
    for copy in act_halo:
        copy.start()
    lax.fori_loop(early, n_tm, lambda j, carry: started(vz_copy)(step_of(j), carry), 0)

    row = lax.broadcasted_iota(jnp.int32, (rows, chans), 0)
    is_first, is_last = row == 0, row == rows - 1
    has_up, has_down = h > 0, h < n_h - 1
    has_side = (block > 0, block < blocks - 1)

    def kept(flag, value):
        return jnp.where(flag, value, jnp.zeros_like(value))

    def shifted(middle, above, below):
        before = jnp.where(is_first, jnp.broadcast_to(above, middle.shape), pltpu.roll(middle, 1, 0))
        after = jnp.where(is_last, jnp.broadcast_to(below, middle.shape), pltpu.roll(middle, rows - 1, 0))
        return before.astype(BF16), after.astype(BF16)

    def with_halo(f, middle_of, got, corner_at, put):
        got_rows, got_cols, got_corner = got
        above = kept(has_up, got_rows[0, f].astype(F32))
        below = kept(has_down, got_rows[1, f].astype(F32))
        for c in range(cols):
            middle = middle_of(c)
            before, after = shifted(middle.astype(F32), above[c : c + 1], below[c : c + 1])
            put(c + 1, before, middle, after)
        for side, c in ((0, 0), (1, cols + 1)):
            middle = kept(has_side[side], got_cols[side, f].astype(F32))
            above_side = kept(has_side[side] & has_up, got_corner[corner_at(2 * side)])
            below_side = kept(has_side[side] & has_down, got_corner[corner_at(2 * side + 1)])
            before, after = shifted(middle, above_side, below_side)
            put(c, before, middle.astype(BF16), after)

    for copy in act_halo:
        copy.wait()

    def slope_pair(t, carry):
        lines = []
        for i in range(pair):
            f = t * pair + i

            def put(c, before, middle, after):
                act[f, c, :, 0:chans] = before
                if c == 0 or c == cols + 1:
                    act[f, c, :, chans : 2 * chans] = middle
                act[f, c, :, 2 * chans : 3 * chans] = after

            with_halo(f, lambda c: act[f, c + 1, :, chans : 2 * chans], act_got, act_corner(f), put)
            lines.append(
                jnp.concatenate([act[f, b : b + cols].reshape(cols * rows, 3 * chans) for b in range(3)], axis=1))
        pre = jnp.dot(jnp.concatenate(lines, axis=0), s_fwd[...], preferred_element_type=F32)
        sig = jax.nn.sigmoid(pre)
        slope[pl.ds(t * pair, pair)] = (sig * (1.0 + pre * (1.0 - sig))).reshape(pair, cols * rows, chans)
        return carry

    lax.fori_loop(0, n_tm, slope_pair, 0)

    def delta_halo(t):
        span = pl.ds(t * pair, pair)
        return halo_copies(
            delta_sent, delta_got, delta.at[span, 0], delta.at[span, cols - 1], span, (t,), d_send.at[t], d_recv.at[t])

    own_grad.wait()

    def delta_pair(j):
        d = step_of(j)
        t = (tm + n_tm - d) % n_tm

        @pl.when(j > 0)
        def _():
            vz_copy(d).wait()

        for i in range(pair):
            f = t * pair + i
            value = (grads[t, :, i].reshape(cols * rows, chans).astype(F32) * slope[f]).astype(BF16)
            delta[f] = value.reshape(cols, rows, chans)
            edges_of(value, delta_sent, delta_corner(t, i), f, i)
        for copy in delta_halo(t):
            copy.start()
        span = pl.ds(t * pair, pair)
        here = delta[span].reshape(pair * cols * rows, chans)
        for b in range(3):
            source = act[span, b : b + cols].reshape(pair * cols * rows, 3 * chans)
            s_total[:, b * 3 * chans : (b + 1) * 3 * chans] += lax.dot_general(
                here, source, (((0,), (0,)), ((), ())), preferred_element_type=F32)

    def back_pair(j):
        t = (tm + n_tm - step_of(j)) % n_tm
        for copy in delta_halo(t):
            copy.wait()
        lines = []
        for i in range(pair):
            f = t * pair + i

            def put(c, before, middle, after):
                wide[i, c, :, 0:chans] = after
                wide[i, c, :, chans : 2 * chans] = middle
                wide[i, c, :, 2 * chans : 3 * chans] = before

            with_halo(f, lambda c: delta[f, c], delta_got, delta_corner(t, i), put)
            lines.append(jnp.concatenate(
                [wide[i, 2 - b : 2 - b + cols].reshape(cols * rows, 3 * chans) for b in range(3)], axis=1))
        value = jnp.dot(jnp.concatenate(lines, axis=0), s_bwd[...], preferred_element_type=F32).astype(BF16)
        act_grad[pl.ds(t * pair, pair)] = value.reshape(pair, cols * rows, chans)

    lag = 3

    def delta_back(j, carry):
        delta_pair(j)

        @pl.when(j >= lag)
        def _():
            back_pair(j - lag)

        return carry

    def back_only(j, carry):
        back_pair(j)
        return carry

    lax.fori_loop(0, n_tm, delta_back, 0)

    def device(t, row_band, core):
        return {"device_id": (t, row_band, core), "device_id_type": MESH}

    def summed_over_all(terms, out, bufs, sems):
        pair_buf, half, h_buf, z_buf = bufs
        swap_sem, h_send, h_recv, z_send, z_recv, g_send, g_recv, f_sem = sems
        taps = half.shape[0]
        piece = chans // n_h
        mine, theirs = pl.ds(w * taps, taps), pl.ds((1 - w) * taps, taps)

        def band(i):
            return pl.ds(pl.multiple_of(i * piece, piece), piece)

        swap = pltpu.make_async_remote_copy(
            src_ref=terms.at[theirs], dst_ref=pair_buf, send_sem=swap_sem.at[0], recv_sem=swap_sem.at[1],
            **device(tm, h, 1 - w))

        def h_copy(d):
            to = (h + d) % n_h
            return pltpu.make_async_remote_copy(
                src_ref=half.at[:, band(to)], dst_ref=h_buf.at[d], send_sem=h_send.at[d], recv_sem=h_recv.at[d],
                **device(tm, to, w))

        def z_copy(d):
            return pltpu.make_async_remote_copy(
                src_ref=z_buf.at[tm], dst_ref=z_buf.at[tm], send_sem=z_send.at[d], recv_sem=z_recv.at[d],
                **device((tm + d) % n_tm, h, w))

        def g_copy(d):
            return pltpu.make_async_remote_copy(
                src_ref=out.at[mine, band(h)], dst_ref=out.at[mine, band(h)], send_sem=g_send.at[d], recv_sem=g_recv.at[d],
                **device(tm, (h + d) % n_h, w))

        share = pltpu.make_async_remote_copy(
            src_ref=out.at[mine], dst_ref=out.at[mine], send_sem=f_sem.at[0], recv_sem=f_sem.at[1],
            **device(tm, h, 1 - w))

        def stage0():
            swap.start()

        def stage1():
            swap.wait()
            half[...] = terms[mine] + pair_buf[...]
            lax.fori_loop(1, n_h, started(h_copy), 0)

        def stage2():
            lax.fori_loop(1, n_h, waited(h_copy), 0)
            total = half[:, band(h), :]
            for d in range(1, n_h):
                total = total + h_buf[d]
            z_buf[tm] = total
            lax.fori_loop(1, n_tm, started(z_copy), 0)

        def stage3():
            lax.fori_loop(1, n_tm, waited(z_copy), 0)
            total = z_buf[0]
            for t in range(1, n_tm):
                total = total + z_buf[t]
            out[mine, band(h), :] = total
            lax.fori_loop(1, n_h, started(g_copy), 0)

        def stage4():
            lax.fori_loop(1, n_h, waited(g_copy), 0)
            share.start()

        def stage5():
            share.wait()

        return stage0, stage1, stage2, stage3, stage4, stage5

    s_terms, t_terms = s_bufs[0], t_bufs[0]
    s_stage = summed_over_all(s_terms, s_out, s_bufs[1:], s_sems)
    t_stage = summed_over_all(t_terms, t_out, t_bufs[1:], t_sems)
    for a in range(3):
        for b in range(3):
            s_terms[a * 3 + b] = s_total[:, (b * 3 + a) * chans : (b * 3 + a + 1) * chans].T * scale
    for k in range(9, s_terms.shape[0]):
        s_terms[k] = jnp.zeros((chans, chans), F32)
    s_stage[0]()

    lax.fori_loop(n_tm - lag, n_tm, back_only, 0)
    s_stage[1]()

    def parts_of(t):
        lines = []
        for i in range(pair):
            f = t * pair + i
            lines.append(jnp.concatenate([
                act_grad[f],
                (act_grad[f + 1].reshape(cols, rows, chans) * mask(f + 1, 1)).reshape(cols * rows, chans),
                (act_grad[f + 2].reshape(cols, rows, chans) * mask(f + 2, 2)).reshape(cols * rows, chans),
            ], axis=1))
        return lines

    def weight_pair(t, carry):
        here = jnp.concatenate(flat([clip[:, t * pair + 2 + i] for i in range(pair)]), axis=0)
        t_total[...] += lax.dot_general(
            here, jnp.concatenate(parts_of(t), axis=0), (((0,), (0,)), ((), ())), preferred_element_type=F32)
        return carry

    def video_pair(t, carry):
        value = jnp.dot(jnp.concatenate(parts_of(t), axis=0), t_bwd[...], preferred_element_type=F32).astype(BF16)
        for i in range(pair):
            moved[:, t * pair + i] = value[i * cols * rows : (i + 1) * cols * rows].reshape(cols, rows, chans)
        return carry

    chunks = o_send.shape[0]
    length = frames // chunks

    def out_place(i):
        return video_grad.at[0, 0, pl.ds(i * length, length), pl.ds(pl.multiple_of(h * rows, rows), rows)]

    def out_copy(i):
        def copy(d):
            to = (h + d) % n_h
            return pltpu.make_async_remote_copy(
                src_ref=moved.at[to, pl.ds(i * length, length)], dst_ref=out_place(i),
                send_sem=o_send.at[i, d], recv_sem=o_recv.at[i, d], **device(tm, to, w))

        return copy

    def own_out(i):
        return pltpu.make_async_copy(moved.at[h, pl.ds(i * length, length)], out_place(i), local_sem.at[5 + i])

    lax.fori_loop(0, n_tm, weight_pair, 0)
    for k in range(3):
        t_terms[k] = t_total[:, k * chans : (k + 1) * chans] * scale
    for k in range(3, t_terms.shape[0]):
        t_terms[k] = jnp.zeros((chans, chans), F32)
    t_stage[0]()
    s_stage[2]()
    between = {0: t_stage[1], 1: s_stage[3], 2: t_stage[2]}
    for i in range(chunks):
        lax.fori_loop(i * n_tm // chunks, (i + 1) * n_tm // chunks, video_pair, 0)
        if i in between:
            between[i]()
        lax.fori_loop(1, n_h, started(out_copy(i)), 0)
        own_out(i).start()
    t_stage[3]()
    s_stage[4]()
    t_stage[4]()
    s_stage[5]()
    for i in range(chunks):
        own_out(i).wait()
        lax.fori_loop(1, n_h, waited(out_copy(i)), 0)
    t_stage[5]()


def shards(n_tm, n_h, n_w, video, out_grad, lengths, temporal_weight, spatial_weight):
    frames, all_rows, chans = video.shape[2:]
    rows = all_rows // n_h
    cols = out_grad.shape[1] // n_tm
    pair = frames // n_tm
    lags = temporal_weight.shape[0]
    offs = spatial_weight.shape[0]
    s_taps = -(-offs * offs // n_w)
    t_taps = -(-lags // n_w)
    chunks = 4
    scale = float(frames * all_rows * cols * n_tm * n_w) ** (-0.5)
    dma = pltpu.SemaphoreType.DMA
    vmem = pltpu.VMEM

    def sum_bufs(taps):
        return [
            vmem((n_w * taps, chans, chans), F32),
            vmem((taps, chans, chans), F32),
            vmem((taps, chans, chans), F32),
            vmem((n_h, taps, chans // n_h, chans), F32),
            vmem((n_tm, taps, chans // n_h, chans), F32),
        ]

    def sum_sems():
        return [dma((2,)), dma((n_h,)), dma((n_h,)), dma((n_tm,)), dma((n_tm,)), dma((n_h,)), dma((n_h,)), dma((2,))]

    hbm = pl.BlockSpec(memory_space=pltpu.HBM)
    video_grad, t_sum, s_sum = pl.pallas_call(
        functools.partial(kernel, n_tm, n_h, n_w, scale),
        out_shape=(
            jax.ShapeDtypeStruct(video.shape, BF16),
            jax.ShapeDtypeStruct((n_w * t_taps, chans, chans), F32),
            jax.ShapeDtypeStruct((n_w * s_taps, chans, chans), F32),
        ),
        in_specs=[hbm] * 5,
        out_specs=(
            pl.BlockSpec(memory_space=pl.ANY), pl.BlockSpec(memory_space=pltpu.VMEM), pl.BlockSpec(memory_space=pltpu.VMEM)),
        scratch_shapes=[
            vmem((cols, frames + 2, rows, chans), BF16),
            vmem((n_tm, cols, pair, rows, chans), BF16),
            vmem((frames, cols + 2, rows, 3 * chans), BF16),
            [vmem((2, frames, cols, chans), BF16), vmem((2, frames, rows, chans), BF16), vmem((4, frames, chans), F32)],
            [vmem((2, frames, cols, chans), BF16), vmem((4, frames, chans), F32)],
            vmem((frames, cols, rows, chans), BF16),
            [vmem((2, frames, cols, chans), BF16), vmem((2, frames, rows, chans), BF16), vmem((4, n_tm, 8, chans), F32)],
            [vmem((2, frames, cols, chans), BF16), vmem((4, n_tm, 8, chans), F32)],
            vmem((frames, cols * rows, chans), F32),
            vmem((frames + 2, cols * rows, chans), BF16),
            vmem((cols, frames, rows, chans), BF16),
            vmem((pair, cols * rows, chans), F32),
            vmem((pair, cols + 2, rows, 3 * chans), BF16),
            vmem((chans, offs * offs * chans), F32),
            vmem((chans, lags * chans), F32),
            sum_bufs(s_taps),
            sum_bufs(t_taps),
            vmem((lags * chans, chans), BF16),
            vmem((lags * chans, chans), BF16),
            vmem((offs * offs * chans, chans), BF16),
            vmem((offs * offs * chans, chans), BF16),
            pltpu.SMEM(lengths.shape, jnp.int32),
            vmem(temporal_weight.shape, BF16),
            vmem(spatial_weight.shape, BF16),
            dma((5 + chunks,)), dma((n_tm,)), dma((n_tm,)), dma((n_h,)), dma((n_h,)), dma((8,)), dma((8,)),
            dma((n_tm, 8)), dma((n_tm, 8)), dma((chunks, n_h)), dma((chunks, n_h)),
            sum_sems(),
            sum_sems(),
        ],
        compiler_params=pltpu.CompilerParams(collective_id=0, has_side_effects=True, vmem_limit_bytes=48 << 20),
    )(video, out_grad, lengths, temporal_weight, spatial_weight)
    return (
        video_grad,
        t_sum[:lags],
        s_sum[: offs * offs].reshape(offs, offs, chans, chans),
    )


def solution(mesh):
    placed = (
        P("width", ("tm", "height"), None, None, None),
        P("width", None, "tm", "height", None),
        P(),
        P(),
        P(),
    )
    return jax.shard_map(
        functools.partial(shards, mesh.shape["tm"], mesh.shape["height"], mesh.shape["width"]),
        mesh=mesh,
        in_specs=placed,
        out_specs=(P("width", ("tm", "height"), None, None, None), P(), P()),
        check_vma=False,
    )
```

time: 111 us -> 107 us (0.964)
  Pallas kernels: 102 us -> 98.8 us
    pallas_call x1, Pallas kernels: 102 us -> 98.8 us  [shards(): pl.pallas_call(functools.partial(kernel, n_tm, n_h, n_w, scale), out_shap...]
where the time goes in v3:
time: 107 us
  Pallas kernels  98.8 us (92%)
  local copies, waits for them, and re-layouts  7.47 us (7%)
    pallas_call x1, Pallas kernels, shards(): pl.pallas_call(functools.partial(kernel, n_tm, n_h, n_w, scale), out_shap...  98.8 us
    unnamed x11, local copies, waits for them, and re-layouts  5.92 us

profile of v3, /device:TPU:1, one launch (start us, length us, event | category | flops | bytes accessed | tf_op | source)
XLA Modules:
  0.0 106.9 jit_solution(17553981367397998756)
XLA Ops:
  0.6 0.0 copy-start
  0.6 1.2 %copy-done = bf16[1,1,16,256,128]{4,3,2,1,0:T(8,128)(2,1)S(1)} copy-done((bf16[1,1,16,256,128]{4,3,2,1,0:T(8,128)(2,1)S(1)}, bf16[1,1,16,256,128]{4,3,2,1,0:T(8,128)(2,1)}, u32[]{:S(2)}) %copy-start) | copy-done | bytes 1048600
  1.9 0.0 copy-start.1
  1.9 1.2 %copy-done.1 = bf16[1,128,2,16,128]{4,3,2,1,0:T(8,128)(2,1)S(1)} copy-done((bf16[1,128,2,16,128]{4,3,2,1,0:T(8,128)(2,1)S(1)}, bf16[1,128,2,16,128]{4,3,2,1,0:T(8,128)(2,1)}, u32[]{:S(2)}) %copy-start.1) | copy-done | bytes 1048600
  3.1 0.0 copy-start.2
  3.1 1.0 copy-done.2
  4.0 0.0 copy-start.3
  4.0 0.9 copy-done.3
  4.9 0.0 copy-start.4
  4.9 0.7 copy-done.4
  5.6 98.8 %shard_map.76 = (bf16[1,1,16,256,128]{4,3,2,1,0:T(8,128)(2,1)S(1)}, f32[4,128,128]{2,1,0:T(8,128)S(1)}, f32[10,128,128]{2,1,0:T(8,128)S(1)}) custom-call(bf16[1,1,16,256,128]{4,3,2,1,0:T(8,128)(2,1)S(1)} %copy-done, bf16[1,128,2,16,128]{4,3,2,1,0:T(8,128)(2,1)S(1)} %copy-done.1, s32[4]{0:T(128)S(1)} %copy-done.4, bf16[3,128,128]{2,1,0:T(8,128)(2,1)S(1)} %copy-done.3, ...), custom_call_target="tpu_custom_call" | custom-call | tf_op jit(solution)/shard_map/pallas_call | solution.py:472
  104.4 0.7 slice.6
  105.1 0.9 slice.7
  106.0 1.0 copy.9
Async XLA Ops:
  0.6 1.2 %copy-start = (bf16[1,1,16,256,128]{4,3,2,1,0:T(8,128)(2,1)S(1)}, bf16[1,1,16,256,128]{4,3,2,1,0:T(8,128)(2,1)}, u32[]{:S(2)}) copy-start(bf16[1,1,16,256,128]{4,3,2,1,0:T(8,128)(2,1)} %video.1) | copy-start | bytes 3145732
  1.9 1.2 %copy-start.1 = (bf16[1,128,2,16,128]{4,3,2,1,0:T(8,128)(2,1)S(1)}, bf16[1,128,2,16,128]{4,3,2,1,0:T(8,128)(2,1)}, u32[]{:S(2)}) copy-start(bf16[1,128,2,16,128]{4,3,2,1,0:T(8,128)(2,1)} %out_grad.1) | copy-start | bytes 3145732
  3.1 1.0 copy-start.2
  4.0 0.9 copy-start.3
  4.9 0.7 copy-start.4

commit v4 on v3

--- a/solution.py
+++ b/solution.py
@@ -91,9 +91,8 @@
     def step_of(j):
         return (((j + 1) // 2) * (2 * (j % 2) - 1) + n_tm) % n_tm
 
-    early = n_tm - 2
     lax.fori_loop(1, n_h, started(vh_copy), 0)
-    lax.fori_loop(1, early, lambda j, carry: started(vz_copy)(step_of(j), carry), 0)
+    lax.fori_loop(1, n_tm, lambda j, carry: started(vz_copy)(step_of(j), carry), 0)
     own_grad = pltpu.make_async_copy(out_grad.at[0, pl.ds(tm * cols, cols)], grads.at[tm], local_sem.at[3])
     own_clip = pltpu.make_async_copy(
         video.at[0, 0, :, pl.ds(pl.multiple_of(h * rows, rows), rows)], clip.at[h, pl.ds(2, frames)], local_sem.at[4])
@@ -175,7 +174,6 @@
         act_sent, act_got, act.at[:, 1, :, mid], act.at[:, cols, :, mid], pl.ds(0, frames), (), a_send, a_recv)
     for copy in act_halo:
         copy.start()
-    lax.fori_loop(early, n_tm, lambda j, carry: started(vz_copy)(step_of(j), carry), 0)
 
     row = lax.broadcasted_iota(jnp.int32, (rows, chans), 0)
     is_first, is_last = row == 0, row == rows - 1
@@ -236,7 +234,7 @@
 
     own_grad.wait()
 
-    def delta_pair(j):
+    def delta_pair(j, carry):
         d = step_of(j)
         t = (tm + n_tm - d) % n_tm
 
@@ -251,14 +249,18 @@
             edges_of(value, delta_sent, delta_corner(t, i), f, i)
         for copy in delta_halo(t):
             copy.start()
+        return carry
+
+    def spatial_pair(t, carry):
         span = pl.ds(t * pair, pair)
         here = delta[span].reshape(pair * cols * rows, chans)
         for b in range(3):
             source = act[span, b : b + cols].reshape(pair * cols * rows, 3 * chans)
             s_total[:, b * 3 * chans : (b + 1) * 3 * chans] += lax.dot_general(
                 here, source, (((0,), (0,)), ((), ())), preferred_element_type=F32)
-
-    def back_pair(j):
+        return carry
+
+    def back_pair(j, carry):
         t = (tm + n_tm - step_of(j)) % n_tm
         for copy in delta_halo(t):
             copy.wait()
@@ -276,29 +278,16 @@
                 [wide[i, 2 - b : 2 - b + cols].reshape(cols * rows, 3 * chans) for b in range(3)], axis=1))
         value = jnp.dot(jnp.concatenate(lines, axis=0), s_bwd[...], preferred_element_type=F32).astype(BF16)
         act_grad[pl.ds(t * pair, pair)] = value.reshape(pair, cols * rows, chans)
-
-    lag = 3
-
-    def delta_back(j, carry):
-        delta_pair(j)
-
-        @pl.when(j >= lag)
-        def _():
-            back_pair(j - lag)
-
-        return carry
-
-    def back_only(j, carry):
-        back_pair(j)
-        return carry
-
-    lax.fori_loop(0, n_tm, delta_back, 0)
+        return carry
+
+    lax.fori_loop(0, n_tm, delta_pair, 0)
+    lax.fori_loop(0, n_tm, spatial_pair, 0)
 
     def device(t, row_band, core):
         return {"device_id": (t, row_band, core), "device_id_type": MESH}
 
     def summed_over_all(terms, out, bufs, sems):
-        pair_buf, half, h_buf, z_buf = bufs
+        pair_buf, half, h_buf, z_buf, got_mine, got_theirs = bufs
         swap_sem, h_send, h_recv, z_send, z_recv, g_send, g_recv, f_sem = sems
         taps = half.shape[0]
         piece = chans // n_h
@@ -324,11 +313,11 @@
 
         def g_copy(d):
             return pltpu.make_async_remote_copy(
-                src_ref=out.at[mine, band(h)], dst_ref=out.at[mine, band(h)], send_sem=g_send.at[d], recv_sem=g_recv.at[d],
+                src_ref=got_mine.at[h], dst_ref=got_mine.at[h], send_sem=g_send.at[d], recv_sem=g_recv.at[d],
                 **device(tm, (h + d) % n_h, w))
 
         share = pltpu.make_async_remote_copy(
-            src_ref=out.at[mine], dst_ref=out.at[mine], send_sem=f_sem.at[0], recv_sem=f_sem.at[1],
+            src_ref=got_mine, dst_ref=got_theirs, send_sem=f_sem.at[0], recv_sem=f_sem.at[1],
             **device(tm, h, 1 - w))
 
         def stage0():
@@ -352,15 +341,19 @@
             total = z_buf[0]
             for t in range(1, n_tm):
                 total = total + z_buf[t]
-            out[mine, band(h), :] = total
+            got_mine[h] = total.astype(BF16)
             lax.fori_loop(1, n_h, started(g_copy), 0)
 
         def stage4():
             lax.fori_loop(1, n_h, waited(g_copy), 0)
             share.start()
+            for i in range(n_h):
+                out[mine, i * piece : (i + 1) * piece, :] = got_mine[i].astype(F32)
 
         def stage5():
             share.wait()
+            for i in range(n_h):
+                out[theirs, i * piece : (i + 1) * piece, :] = got_theirs[i].astype(F32)
 
         return stage0, stage1, stage2, stage3, stage4, stage5
 
@@ -374,8 +367,9 @@
         s_terms[k] = jnp.zeros((chans, chans), F32)
     s_stage[0]()
 
-    lax.fori_loop(n_tm - lag, n_tm, back_only, 0)
+    lax.fori_loop(0, n_tm // 2, back_pair, 0)
     s_stage[1]()
+    lax.fori_loop(n_tm // 2, n_tm, back_pair, 0)
 
     def parts_of(t):
         lines = []
@@ -418,24 +412,25 @@
     def own_out(i):
         return pltpu.make_async_copy(moved.at[h, pl.ds(i * length, length)], out_place(i), local_sem.at[5 + i])
 
-    lax.fori_loop(0, n_tm, weight_pair, 0)
+    lax.fori_loop(0, n_tm // 2, weight_pair, 0)
+    s_stage[2]()
+    lax.fori_loop(n_tm // 2, n_tm, weight_pair, 0)
     for k in range(3):
         t_terms[k] = t_total[:, k * chans : (k + 1) * chans] * scale
     for k in range(3, t_terms.shape[0]):
         t_terms[k] = jnp.zeros((chans, chans), F32)
     t_stage[0]()
-    s_stage[2]()
-    between = {0: t_stage[1], 1: s_stage[3], 2: t_stage[2]}
+    between = {0: s_stage[3], 1: t_stage[1], 3: t_stage[2]}
     for i in range(chunks):
         lax.fori_loop(i * n_tm // chunks, (i + 1) * n_tm // chunks, video_pair, 0)
         if i in between:
             between[i]()
         lax.fori_loop(1, n_h, started(out_copy(i)), 0)
         own_out(i).start()
+    s_stage[4]()
     t_stage[3]()
-    s_stage[4]()
+    s_stage[5]()
     t_stage[4]()
-    s_stage[5]()
     for i in range(chunks):
         own_out(i).wait()
         lax.fori_loop(1, n_h, waited(out_copy(i)), 0)
@@ -463,6 +458,8 @@
             vmem((taps, chans, chans), F32),
             vmem((n_h, taps, chans // n_h, chans), F32),
             vmem((n_tm, taps, chans // n_h, chans), F32),
+            vmem((n_h, taps, chans // n_h, chans), BF16),
+            vmem((n_h, taps, chans // n_h, chans), BF16),
         ]
 
     def sum_sems():
@@ -509,7 +506,7 @@
             sum_sems(),
             sum_sems(),
         ],
-        compiler_params=pltpu.CompilerParams(collective_id=0, has_side_effects=True, vmem_limit_bytes=48 << 20),
+        compiler_params=pltpu.CompilerParams(collective_id=0, has_side_effects=True, vmem_limit_bytes=54 << 20),
     )(video, out_grad, lengths, temporal_weight, spatial_weight)
     return (
         video_grad,

time: 107 us -> 97.7 us (0.913)
  Pallas kernels: 98.8 us -> 92.3 us
  local copies, waits for them, and re-layouts: 7.47 us -> 4.59 us
    pallas_call x1, Pallas kernels: 98.8 us -> 92.3 us  [shards(): pl.pallas_call(functools.partial(kernel, n_tm, n_h, n_w, scale), out_shap...]
    unnamed x11 -> x3, local copies, waits for them, and re-layouts: 5.92 us -> 0.97 us
where the time goes in v4:
time: 97.7 us; the launch traced here: 97.5 us
  Pallas kernels  92.3 us (94%)
  local copies, waits for them, and re-layouts  4.59 us (5%)
    pallas_call x1, Pallas kernels, shards(): pl.pallas_call(functools.partial(kernel, n_tm, n_h, n_w, scale), out_shap...  92.3 us

profile of v4, /device:TPU:1, one launch (start us, length us, event | category | flops | bytes accessed | tf_op | source)
XLA Modules:
  0.0 97.5 jit_solution(1210213360896958541)
XLA Ops:
  0.6 92.3 %shard_map.76 = (bf16[1,1,16,256,128]{4,3,2,1,0:T(8,128)(2,1)}, f32[4,128,128]{2,1,0:T(8,128)}, f32[10,128,128]{2,1,0:T(8,128)}) custom-call(bf16[1,1,16,256,128]{4,3,2,1,0:T(8,128)(2,1)} %video.1, bf16[1,128,2,16,128]{4,3,2,1,0:T(8,128)(2,1)} %out_grad.1, s32[4]{0:T(128)} %lengths_in.1, bf16[3,128,128]{2,1,0:T(8,128)(2,1)} %t_weight_in.1, ...), custom_call_target="tpu_custom_call" | custom-call | tf_op jit(solution)/shard_map/pallas_call | solution.py:469
  92.9 0.0 copy-start
  92.9 1.7 %slice.6 = f32[3,128,128]{2,1,0:T(8,128)} slice(f32[4,128,128]{2,1,0:T(8,128)} %get-tuple-element.7), slice={[0:3], [0:128], [0:128]} | slice | bytes 393216 | tf_op jit(solution)/shard_map/slice | solution.py:513
  94.6 1.9 %slice.7 = f32[9,128,128]{2,1,0:T(8,128)} slice(f32[10,128,128]{2,1,0:T(8,128)} %get-tuple-element.8), slice={[0:9], [0:128], [0:128]} | slice | bytes 1179648 | tf_op jit(solution)/shard_map/slice | solution.py:514
  96.6 0.0 copy-done
  96.6 1.0 copy.9
Async XLA Ops:
  92.9 3.6 %copy-start = (bf16[1,1,16,256,128]{4,3,2,1,0:T(8,128)(2,1)S(1)}, bf16[1,1,16,256,128]{4,3,2,1,0:T(8,128)(2,1)}, u32[]{:S(2)}) copy-start(bf16[1,1,16,256,128]{4,3,2,1,0:T(8,128)(2,1)} %get-tuple-element.12) | copy-start | bytes 3145732

commit v5 on v4

--- a/solution.py
+++ b/solution.py
@@ -260,8 +260,7 @@
                 here, source, (((0,), (0,)), ((), ())), preferred_element_type=F32)
         return carry
 
-    def back_pair(j, carry):
-        t = (tm + n_tm - step_of(j)) % n_tm
+    def back_pair(t):
         for copy in delta_halo(t):
             copy.wait()
         lines = []
@@ -278,7 +277,6 @@
                 [wide[i, 2 - b : 2 - b + cols].reshape(cols * rows, 3 * chans) for b in range(3)], axis=1))
         value = jnp.dot(jnp.concatenate(lines, axis=0), s_bwd[...], preferred_element_type=F32).astype(BF16)
         act_grad[pl.ds(t * pair, pair)] = value.reshape(pair, cols * rows, chans)
-        return carry
 
     lax.fori_loop(0, n_tm, delta_pair, 0)
     lax.fori_loop(0, n_tm, spatial_pair, 0)
@@ -367,10 +365,6 @@
         s_terms[k] = jnp.zeros((chans, chans), F32)
     s_stage[0]()
 
-    lax.fori_loop(0, n_tm // 2, back_pair, 0)
-    s_stage[1]()
-    lax.fori_loop(n_tm // 2, n_tm, back_pair, 0)
-
     def parts_of(t):
         lines = []
         for i in range(pair):
@@ -382,16 +376,21 @@
             ], axis=1))
         return lines
 
-    def weight_pair(t, carry):
+    def time_pair(t):
         here = jnp.concatenate(flat([clip[:, t * pair + 2 + i] for i in range(pair)]), axis=0)
-        t_total[...] += lax.dot_general(
-            here, jnp.concatenate(parts_of(t), axis=0), (((0,), (0,)), ((), ())), preferred_element_type=F32)
-        return carry
-
-    def video_pair(t, carry):
-        value = jnp.dot(jnp.concatenate(parts_of(t), axis=0), t_bwd[...], preferred_element_type=F32).astype(BF16)
+        parts = jnp.concatenate(parts_of(t), axis=0)
+        t_total[...] += lax.dot_general(here, parts, (((0,), (0,)), ((), ())), preferred_element_type=F32)
+        value = jnp.dot(parts, t_bwd[...], preferred_element_type=F32).astype(BF16)
         for i in range(pair):
             moved[:, t * pair + i] = value[i * cols * rows : (i + 1) * cols * rows].reshape(cols, rows, chans)
+
+    def back_time(t, carry):
+        back_pair(t)
+
+        @pl.when(t >= 1)
+        def _():
+            time_pair(t - 1)
+
         return carry
 
     chunks = o_send.shape[0]
@@ -412,25 +411,32 @@
     def own_out(i):
         return pltpu.make_async_copy(moved.at[h, pl.ds(i * length, length)], out_place(i), local_sem.at[5 + i])
 
-    lax.fori_loop(0, n_tm // 2, weight_pair, 0)
-    s_stage[2]()
-    lax.fori_loop(n_tm // 2, n_tm, weight_pair, 0)
+    def send_back(i):
+        lax.fori_loop(1, n_h, started(out_copy(i)), 0)
+        own_out(i).start()
+
+    after = {0: s_stage[1], 2: s_stage[2]}
+    per = n_tm // chunks
+    for i in range(chunks):
+        lax.fori_loop(i * per + (i > 0), min((i + 1) * per + 1, n_tm), back_time, 0)
+        if i in after:
+            after[i]()
+        if i < chunks - 1:
+            send_back(i)
+    time_pair(n_tm - 1)
     for k in range(3):
         t_terms[k] = t_total[:, k * chans : (k + 1) * chans] * scale
     for k in range(3, t_terms.shape[0]):
         t_terms[k] = jnp.zeros((chans, chans), F32)
     t_stage[0]()
-    between = {0: s_stage[3], 1: t_stage[1], 3: t_stage[2]}
-    for i in range(chunks):
-        lax.fori_loop(i * n_tm // chunks, (i + 1) * n_tm // chunks, video_pair, 0)
-        if i in between:
-            between[i]()
-        lax.fori_loop(1, n_h, started(out_copy(i)), 0)
-        own_out(i).start()
+    t_stage[1]()
+    t_stage[2]()
+    send_back(chunks - 1)
+    s_stage[3]()
+    t_stage[3]()
     s_stage[4]()
-    t_stage[3]()
+    t_stage[4]()
     s_stage[5]()
-    t_stage[4]()
     for i in range(chunks):
         own_out(i).wait()
         lax.fori_loop(1, n_h, waited(out_copy(i)), 0)

time: 97.7 us -> 91.4 us (0.936)
  Pallas kernels: 92.3 us -> 86 us
    pallas_call x1, Pallas kernels: 92.3 us -> 86 us  [shards(): pl.pallas_call(functools.partial(kernel, n_tm, n_h, n_w, scale), out_shap...]
where the time goes in v5:
time: 91.4 us; the launch traced here: 91.2 us
  Pallas kernels  86 us (94%)
  local copies, waits for them, and re-layouts  4.59 us (5%)
    pallas_call x1, Pallas kernels, shards(): pl.pallas_call(functools.partial(kernel, n_tm, n_h, n_w, scale), out_shap...  86 us
    slice x1, local copies, waits for them, and re-layouts, shards(): s_sum[:offs * offs].reshape(offs, offs, chans, chans)  1.92 us

profile of v5, /device:TPU:1, one launch (start us, length us, event | category | flops | bytes accessed | tf_op | source)
XLA Modules:
  0.0 91.2 jit_solution(2443139804305409092)
XLA Ops:
  0.6 86.0 %shard_map.76 = (bf16[1,1,16,256,128]{4,3,2,1,0:T(8,128)(2,1)}, f32[4,128,128]{2,1,0:T(8,128)}, f32[10,128,128]{2,1,0:T(8,128)}) custom-call(bf16[1,1,16,256,128]{4,3,2,1,0:T(8,128)(2,1)} %video.1, bf16[1,128,2,16,128]{4,3,2,1,0:T(8,128)(2,1)} %out_grad.1, s32[4]{0:T(128)} %lengths_in.1, bf16[3,128,128]{2,1,0:T(8,128)(2,1)} %t_weight_in.1, ...), custom_call_target="tpu_custom_call" | custom-call | tf_op jit(solution)/shard_map/pallas_call | solution.py:475
  86.6 0.0 copy-start
  86.6 1.7 %slice.6 = f32[3,128,128]{2,1,0:T(8,128)} slice(f32[4,128,128]{2,1,0:T(8,128)} %get-tuple-element.7), slice={[0:3], [0:128], [0:128]} | slice | bytes 393216 | tf_op jit(solution)/shard_map/slice | solution.py:519
  88.3 1.9 %slice.7 = f32[9,128,128]{2,1,0:T(8,128)} slice(f32[10,128,128]{2,1,0:T(8,128)} %get-tuple-element.8), slice={[0:9], [0:128], [0:128]} | slice | bytes 1179648 | tf_op jit(solution)/shard_map/slice | solution.py:520
  90.2 0.0 copy-done
  90.2 1.0 %copy.9 = bf16[1,1,16,256,128]{4,3,2,1,0:T(8,128)(2,1)} copy(bf16[1,1,16,256,128]{4,3,2,1,0:T(8,128)(2,1)S(1)} %copy-done) | data formatting | bytes 2097152
Async XLA Ops:
  86.6 3.6 %copy-start = (bf16[1,1,16,256,128]{4,3,2,1,0:T(8,128)(2,1)S(1)}, bf16[1,1,16,256,128]{4,3,2,1,0:T(8,128)(2,1)}, u32[]{:S(2)}) copy-start(bf16[1,1,16,256,128]{4,3,2,1,0:T(8,128)(2,1)} %get-tuple-element.12) | copy-start | bytes 3145732

commit v6 on v5

--- a/solution.py
+++ b/solution.py
@@ -31,9 +31,9 @@
 def kernel(
     n_tm, n_h, n_w, scale,
     video, out_grad, lengths_in, t_weight_in, s_weight_in,
-    video_grad, t_out, s_out,
-    clip, grads, act, act_got, act_sent, delta, delta_got, delta_sent,
-    slope, act_grad, moved, plane, wide, s_total, t_total, s_bufs, t_bufs,
+    video_grad, t_sum, s_sum,
+    clip, grads, act, act_side, act_got, act_sent, delta, delta_got, delta_sent,
+    slope, act_grad, moved, plane, wide, s_total, t_total, s_bufs, t_bufs, s_out, t_out,
     t_fwd, t_bwd, s_fwd, s_bwd, lengths, t_weight, s_weight,
     local_sem, vz_send, vz_recv, vh_send, vh_recv, a_send, a_recv, d_send, d_recv, o_send, o_recv, s_sems, t_sems,
 ):
@@ -82,16 +82,24 @@
             src_ref=out_grad.at[0, pl.ds(to * cols, cols)], dst_ref=grads.at[tm],
             send_sem=vz_send.at[d], recv_sem=vz_recv.at[d], device_id=(to, h, w), device_id_type=MESH)
 
-    def vh_copy(d):
-        to = (h + d) % n_h
-        return pltpu.make_async_remote_copy(
-            src_ref=video.at[0, 0, :, pl.ds(pl.multiple_of(to * rows, rows), rows)], dst_ref=clip.at[h, pl.ds(2, frames)],
-            send_sem=vh_send.at[d], recv_sem=vh_recv.at[d], device_id=(tm, to, w), device_id_type=MESH)
+    parts_in = vh_send.shape[0]
+    run = frames // parts_in
+
+    def vh_copy(i):
+        def copy(d):
+            to = (h + d) % n_h
+            return pltpu.make_async_remote_copy(
+                src_ref=video.at[0, 0, pl.ds(i * run, run), pl.ds(pl.multiple_of(to * rows, rows), rows)],
+                dst_ref=clip.at[h, pl.ds(2 + i * run, run)],
+                send_sem=vh_send.at[i, d], recv_sem=vh_recv.at[i, d], device_id=(tm, to, w), device_id_type=MESH)
+
+        return copy
 
     def step_of(j):
         return (((j + 1) // 2) * (2 * (j % 2) - 1) + n_tm) % n_tm
 
-    lax.fori_loop(1, n_h, started(vh_copy), 0)
+    for i in range(parts_in):
+        lax.fori_loop(1, n_h, started(vh_copy(i)), 0)
     lax.fori_loop(1, n_tm, lambda j, carry: started(vz_copy)(step_of(j), carry), 0)
     own_grad = pltpu.make_async_copy(out_grad.at[0, pl.ds(tm * cols, cols)], grads.at[tm], local_sem.at[3])
     own_clip = pltpu.make_async_copy(
@@ -124,7 +132,6 @@
         return jnp.broadcast_to(keep.astype(F32), (rows, chans)).astype(BF16)[None]
 
     own_clip.wait()
-    lax.fori_loop(1, n_h, waited(vh_copy), 0)
 
     def edges_of(value, sent, corner_at, f, i):
         edge, corner = sent
@@ -152,10 +159,10 @@
         for i in range(pair):
             value = both[i * cols * rows : (i + 1) * cols * rows]
             act[t * pair + i, 1 : cols + 1, :, chans : 2 * chans] = value.reshape(cols, rows, chans)
+            act_side[0, t * pair + i] = value[:rows]
+            act_side[1, t * pair + i] = value[(cols - 1) * rows :]
             edges_of(value, act_sent, act_corner(t * pair + i), t * pair + i, i)
         return carry
-
-    lax.fori_loop(0, n_tm, act_pair, 0)
 
     def halo_copies(sent, got, first, last, span, part, send, recv):
         (edge, corner), (got_rows, got_cols, got_corner) = sent, got
@@ -169,11 +176,16 @@
             for i, (src, dst) in enumerate(parts)
         ]
 
-    mid = pl.ds(chans, chans)
-    act_halo = halo_copies(
-        act_sent, act_got, act.at[:, 1, :, mid], act.at[:, cols, :, mid], pl.ds(0, frames), (), a_send, a_recv)
-    for copy in act_halo:
-        copy.start()
+    def act_halo(i):
+        span = pl.ds(i * run, run)
+        return halo_copies(
+            act_sent, act_got, act_side.at[0, span], act_side.at[1, span], span, (span,), a_send.at[i], a_recv.at[i])
+
+    for i in range(parts_in):
+        lax.fori_loop(1, n_h, waited(vh_copy(i)), 0)
+        lax.fori_loop(i * run // pair, (i + 1) * run // pair, act_pair, 0)
+        for copy in act_halo(i):
+            copy.start()
 
     row = lax.broadcasted_iota(jnp.int32, (rows, chans), 0)
     is_first, is_last = row == 0, row == rows - 1
@@ -203,8 +215,6 @@
             before, after = shifted(middle, above_side, below_side)
             put(c, before, middle.astype(BF16), after)
 
-    for copy in act_halo:
-        copy.wait()
 
     def slope_pair(t, carry):
         lines = []
@@ -225,7 +235,10 @@
         slope[pl.ds(t * pair, pair)] = (sig * (1.0 + pre * (1.0 - sig))).reshape(pair, cols * rows, chans)
         return carry
 
-    lax.fori_loop(0, n_tm, slope_pair, 0)
+    for i in range(parts_in):
+        for copy in act_halo(i):
+            copy.wait()
+        lax.fori_loop(i * run // pair, (i + 1) * run // pair, slope_pair, 0)
 
     def delta_halo(t):
         span = pl.ds(t * pair, pair)
@@ -251,11 +264,11 @@
             copy.start()
         return carry
 
-    def spatial_pair(t, carry):
-        span = pl.ds(t * pair, pair)
-        here = delta[span].reshape(pair * cols * rows, chans)
+    def spatial_part(t, carry):
+        span = pl.ds(t * 2 * pair, 2 * pair)
+        here = delta[span].reshape(2 * pair * cols * rows, chans)
         for b in range(3):
-            source = act[span, b : b + cols].reshape(pair * cols * rows, 3 * chans)
+            source = act[span, b : b + cols].reshape(2 * pair * cols * rows, 3 * chans)
             s_total[:, b * 3 * chans : (b + 1) * 3 * chans] += lax.dot_general(
                 here, source, (((0,), (0,)), ((), ())), preferred_element_type=F32)
         return carry
@@ -279,7 +292,7 @@
         act_grad[pl.ds(t * pair, pair)] = value.reshape(pair, cols * rows, chans)
 
     lax.fori_loop(0, n_tm, delta_pair, 0)
-    lax.fori_loop(0, n_tm, spatial_pair, 0)
+    lax.fori_loop(0, n_tm // 2, spatial_part, 0)
 
     def device(t, row_band, core):
         return {"device_id": (t, row_band, core), "device_id_type": MESH}
@@ -317,6 +330,11 @@
         share = pltpu.make_async_remote_copy(
             src_ref=got_mine, dst_ref=got_theirs, send_sem=f_sem.at[0], recv_sem=f_sem.at[1],
             **device(tm, h, 1 - w))
+
+        def gather(place, got):
+            for i in range(0, n_h, 2):
+                both = jnp.concatenate([got[i].astype(F32), got[i + 1].astype(F32)], axis=1)
+                out[place, i * piece : (i + 2) * piece, :] = both.astype(BF16)
 
         def stage0():
             swap.start()
@@ -345,13 +363,11 @@
         def stage4():
             lax.fori_loop(1, n_h, waited(g_copy), 0)
             share.start()
-            for i in range(n_h):
-                out[mine, i * piece : (i + 1) * piece, :] = got_mine[i].astype(F32)
+            gather(mine, got_mine)
 
         def stage5():
             share.wait()
-            for i in range(n_h):
-                out[theirs, i * piece : (i + 1) * piece, :] = got_theirs[i].astype(F32)
+            gather(theirs, got_theirs)
 
         return stage0, stage1, stage2, stage3, stage4, stage5
 
@@ -376,10 +392,13 @@
             ], axis=1))
         return lines
 
-    def time_pair(t):
+    def weight_pair(t):
         here = jnp.concatenate(flat([clip[:, t * pair + 2 + i] for i in range(pair)]), axis=0)
         parts = jnp.concatenate(parts_of(t), axis=0)
         t_total[...] += lax.dot_general(here, parts, (((0,), (0,)), ((), ())), preferred_element_type=F32)
+        return parts
+
+    def video_pair(t, parts):
         value = jnp.dot(parts, t_bwd[...], preferred_element_type=F32).astype(BF16)
         for i in range(pair):
             moved[:, t * pair + i] = value[i * cols * rows : (i + 1) * cols * rows].reshape(cols, rows, chans)
@@ -389,7 +408,7 @@
 
         @pl.when(t >= 1)
         def _():
-            time_pair(t - 1)
+            video_pair(t - 1, weight_pair(t - 1))
 
         return carry
 
@@ -423,12 +442,13 @@
             after[i]()
         if i < chunks - 1:
             send_back(i)
-    time_pair(n_tm - 1)
+    last_parts = weight_pair(n_tm - 1)
     for k in range(3):
         t_terms[k] = t_total[:, k * chans : (k + 1) * chans] * scale
     for k in range(3, t_terms.shape[0]):
         t_terms[k] = jnp.zeros((chans, chans), F32)
     t_stage[0]()
+    video_pair(n_tm - 1, last_parts)
     t_stage[1]()
     t_stage[2]()
     send_back(chunks - 1)
@@ -437,10 +457,12 @@
     s_stage[4]()
     t_stage[4]()
     s_stage[5]()
+    s_sum[...] = s_out[0 : s_sum.shape[0]]
     for i in range(chunks):
         own_out(i).wait()
         lax.fori_loop(1, n_h, waited(out_copy(i)), 0)
     t_stage[5]()
+    t_sum[...] = t_out[0 : t_sum.shape[0]]
 
 
 def shards(n_tm, n_h, n_w, video, out_grad, lengths, temporal_weight, spatial_weight):
@@ -476,8 +498,8 @@
         functools.partial(kernel, n_tm, n_h, n_w, scale),
         out_shape=(
             jax.ShapeDtypeStruct(video.shape, BF16),
-            jax.ShapeDtypeStruct((n_w * t_taps, chans, chans), F32),
-            jax.ShapeDtypeStruct((n_w * s_taps, chans, chans), F32),
+            jax.ShapeDtypeStruct((lags, chans, chans), BF16),
+            jax.ShapeDtypeStruct((offs * offs, chans, chans), BF16),
         ),
         in_specs=[hbm] * 5,
         out_specs=(
@@ -486,6 +508,7 @@
             vmem((cols, frames + 2, rows, chans), BF16),
             vmem((n_tm, cols, pair, rows, chans), BF16),
             vmem((frames, cols + 2, rows, 3 * chans), BF16),
+            vmem((2, frames, rows, chans), BF16),
             [vmem((2, frames, cols, chans), BF16), vmem((2, frames, rows, chans), BF16), vmem((4, frames, chans), F32)],
             [vmem((2, frames, cols, chans), BF16), vmem((4, frames, chans), F32)],
             vmem((frames, cols, rows, chans), BF16),
@@ -500,6 +523,8 @@
             vmem((chans, lags * chans), F32),
             sum_bufs(s_taps),
             sum_bufs(t_taps),
+            vmem((n_w * s_taps, chans, chans), BF16),
+            vmem((n_w * t_taps, chans, chans), BF16),
             vmem((lags * chans, chans), BF16),
             vmem((lags * chans, chans), BF16),
             vmem((offs * offs * chans, chans), BF16),
@@ -507,7 +532,7 @@
             pltpu.SMEM(lengths.shape, jnp.int32),
             vmem(temporal_weight.shape, BF16),
             vmem(spatial_weight.shape, BF16),
-            dma((5 + chunks,)), dma((n_tm,)), dma((n_tm,)), dma((n_h,)), dma((n_h,)), dma((8,)), dma((8,)),
+            dma((5 + chunks,)), dma((n_tm,)), dma((n_tm,)), dma((2, n_h)), dma((2, n_h)), dma((2, 8)), dma((2, 8)),
             dma((n_tm, 8)), dma((n_tm, 8)), dma((chunks, n_h)), dma((chunks, n_h)),
             sum_sems(),
             sum_sems(),
@@ -516,8 +541,8 @@
     )(video, out_grad, lengths, temporal_weight, spatial_weight)
     return (
         video_grad,
-        t_sum[:lags],
-        s_sum[: offs * offs].reshape(offs, offs, chans, chans),
+        t_sum.astype(F32),
+        s_sum.astype(F32).reshape(offs, offs, chans, chans),
     )
 
 

time: 91.4 us -> 90.6 us (level)
  local copies, waits for them, and re-layouts: 4.59 us -> 0.97 us
  other arithmetic: 0 us -> 3.49 us
    slice x2 -> x0, local copies, waits for them, and re-layouts: 3.62 us -> none  [the longest x1 1.92 us: shards(): s_sum[:offs * offs].reshape(offs, offs, chans, chans)]
    reshape x0 -> x1, other arithmetic: none -> 1.82 us  [shards(): s_sum.astype(F32).reshape(offs, offs, chans, chans)]
    convert_element_type x0 -> x1, other arithmetic: none -> 1.67 us  [shards(): t_sum.astype(F32)]
where the time goes in v6:
time: 90.6 us; the launch traced here: 90.5 us
  Pallas kernels  85.4 us (94%)
  other arithmetic  3.49 us (4%)
  local copies, waits for them, and re-layouts  0.97 us (1%)
    pallas_call x1, Pallas kernels, shards(): pl.pallas_call(functools.partial(kernel, n_tm, n_h, n_w, scale), out_shap...  85.4 us
    reshape x1, other arithmetic, shards(): s_sum.astype(F32).reshape(offs, offs, chans, chans)  1.82 us

profile of v6, /device:TPU:1, one launch (start us, length us, event | category | flops | bytes accessed | tf_op | source)
XLA Modules:
  0.0 90.5 jit_solution(17861111546597842484)
XLA Ops:
  0.6 85.4 %shard_map.76 = (bf16[1,1,16,256,128]{4,3,2,1,0:T(8,128)(2,1)}, bf16[3,128,128]{2,1,0:T(8,128)(2,1)}, bf16[9,128,128]{2,1,0:T(8,128)(2,1)}) custom-call(bf16[1,1,16,256,128]{4,3,2,1,0:T(8,128)(2,1)} %video.1, bf16[1,128,2,16,128]{4,3,2,1,0:T(8,128)(2,1)} %out_grad.1, s32[4]{0:T(128)} %lengths_in.1, bf16[3,128,128]{2,1,0:T(8,128)(2,1)} %t_weight_in.1, ...), custom_call_target="tpu_custom_call" | custom-call | tf_op jit(solution)/shard_map/pallas_call | solution.py:497
  86.0 0.0 copy-start
  86.0 1.7 %convert_element_type.4 = f32[3,128,128]{2,1,0:T(8,128)} convert(bf16[3,128,128]{2,1,0:T(8,128)(2,1)} %get-tuple-element.7) | non-fusion elementwise | flops 49152 | bytes 294912 | tf_op jit(solution)/shard_map/convert_element_type | solution.py:544
  87.7 1.8 %convert.1 = f32[3,3,128,128]{3,2,1,0:T(8,128)} convert(bf16[3,3,128,128]{3,2,1,0:T(8,128)(2,1)} %bitcast.2) | non-fusion elementwise | flops 147456 | bytes 884736 | tf_op jit(solution)/shard_map/reshape | solution.py:545
  89.5 0.0 copy-done
  89.5 1.0 %copy.9 = bf16[1,1,16,256,128]{4,3,2,1,0:T(8,128)(2,1)} copy(bf16[1,1,16,256,128]{4,3,2,1,0:T(8,128)(2,1)S(1)} %copy-done) | data formatting | bytes 2097152
Async XLA Ops:
  86.0 3.5 %copy-start = (bf16[1,1,16,256,128]{4,3,2,1,0:T(8,128)(2,1)S(1)}, bf16[1,1,16,256,128]{4,3,2,1,0:T(8,128)(2,1)}, u32[]{:S(2)}) copy-start(bf16[1,1,16,256,128]{4,3,2,1,0:T(8,128)(2,1)} %get-tuple-element.12) | copy-start | bytes 3145732

commit v7 on v6

--- a/solution.py
+++ b/solution.py
@@ -537,7 +537,7 @@
             sum_sems(),
             sum_sems(),
         ],
-        compiler_params=pltpu.CompilerParams(collective_id=0, has_side_effects=True, vmem_limit_bytes=54 << 20),
+        compiler_params=pltpu.CompilerParams(collective_id=0, has_side_effects=True, vmem_limit_bytes=54528 << 10),
     )(video, out_grad, lengths, temporal_weight, spatial_weight)
     return (
         video_grad,

time: 90.6 us -> 89.4 us (0.987)
  other arithmetic: 3.49 us -> 1.55 us
  local copies, waits for them, and re-layouts: 0.97 us -> 2.51 us
    unnamed x3 -> x7, local copies, waits for them, and re-layouts: 0.97 us -> 2.51 us
    convert_element_type x1, other arithmetic: 1.67 us -> 0.69 us  [shards(): t_sum.astype(F32)]
    reshape x1, other arithmetic: 1.82 us -> 0.86 us  [shards(): s_sum.astype(F32).reshape(offs, offs, chans, chans)]
where the time goes in v7:
time: 89.4 us; the launch traced here: 89.3 us
  Pallas kernels  84.6 us (95%)
  local copies, waits for them, and re-layouts  2.51 us (3%)
  other arithmetic  1.55 us (2%)
    pallas_call x1, Pallas kernels, shards(): pl.pallas_call(functools.partial(kernel, n_tm, n_h, n_w, scale), out_shap...  84.6 us
    unnamed x7, local copies, waits for them, and re-layouts  2.51 us

profile of v7, /device:TPU:1, one launch (start us, length us, event | category | flops | bytes accessed | tf_op | source)
XLA Modules:
  0.0 89.3 jit_solution(10133821584528271854)
XLA Ops:
  0.6 0.0 copy-start
  0.6 0.9 copy-done
  1.5 0.0 copy-start.1
  1.5 0.7 copy-done.1
  2.2 84.6 %shard_map.76 = (bf16[1,1,16,256,128]{4,3,2,1,0:T(8,128)(2,1)}, bf16[3,128,128]{2,1,0:T(8,128)(2,1)S(1)}, bf16[9,128,128]{2,1,0:T(8,128)(2,1)S(1)}) custom-call(bf16[1,1,16,256,128]{4,3,2,1,0:T(8,128)(2,1)} %video.1, bf16[1,128,2,16,128]{4,3,2,1,0:T(8,128)(2,1)} %out_grad.1, s32[4]{0:T(128)S(1)} %copy-done.1, bf16[3,128,128]{2,1,0:T(8,128)(2,1)S(1)} %copy-done, ...), custom_call_target="tpu_custom_call" | custom-call | tf_op jit(solution)/shard_map/pallas_call | solution.py:497
  86.8 0.0 copy-start.2
  86.8 0.7 convert_element_type.4
  87.5 0.9 convert.1
  88.3 0.0 copy-done.2
  88.3 1.0 %copy.9 = bf16[1,1,16,256,128]{4,3,2,1,0:T(8,128)(2,1)} copy(bf16[1,1,16,256,128]{4,3,2,1,0:T(8,128)(2,1)S(1)} %copy-done.2) | data formatting | bytes 2097152
Async XLA Ops:
  0.6 0.9 %copy-start = (bf16[3,128,128]{2,1,0:T(8,128)(2,1)S(1)}, bf16[3,128,128]{2,1,0:T(8,128)(2,1)}, u32[]{:S(2)}) copy-start(bf16[3,128,128]{2,1,0:T(8,128)(2,1)} %t_weight_in.1) | copy-start | bytes 294916
  1.5 0.7 copy-start.1
  86.8 1.6 %copy-start.2 = (bf16[1,1,16,256,128]{4,3,2,1,0:T(8,128)(2,1)S(1)}, bf16[1,1,16,256,128]{4,3,2,1,0:T(8,128)(2,1)}, u32[]{:S(2)}) copy-start(bf16[1,1,16,256,128]{4,3,2,1,0:T(8,128)(2,1)} %get-tuple-element.12) | copy-start | bytes 3145732
